TPU v7x, 32 devices: a whole 2x2x4 slice. The times are simulated.
32 devices in a mesh: parts: 2 (over y), ctx: 4 (over z), head: 2 (over x), rep: 2 (over core).
Axes of the slice: x: 2, y: 2, z: 4, core: 2. Of those that a mesh axis runs over, the one named last changes fastest.
Arguments:
- query_rows: bfloat16 [4096, 8, 6, 128], P(('parts', 'ctx'), 'head', 'rep'), parts along dimension 0, may hold values from -125 to 125
- key_rows: bfloat16 [4096, 8, 128], P(('parts', 'ctx'), 'head'), parts along dimension 0, may hold values from -5 to 5
- value_rows: bfloat16 [4096, 8, 128], P(('parts', 'ctx'), 'head'), parts along dimension 0, may hold values from -6 to 6
- dest_block: int32 [32], P('parts'), parts along dimension 0, may hold values from 0 to 15, as said below
- tile_list: int32 [32, 4], P('parts'), parts along dimension 0, may hold values from 0 to 15, as said below
- tile_count: int32 [32], P('parts'), parts along dimension 0, may hold values from 1 to 4
- stripe_start: int32 [16, 4], P(('parts', 'head')), parts along dimension 0, may hold values from 0 to 1536, as said below
Outputs:
- attended: bfloat16 [4096, 8, 6, 128], P(('parts', 'ctx'), 'head', 'rep'), parts along dimension 0
There are 2 independent parts, one for each index of `parts`. A program takes and returns all parts, laid end to end along the dimension named above; each array names one. Nothing has to cross between parts.
Inputs may be any that keep to these rules, and one draw needn't show every extreme that they name: dest_block is a permutation of the blocks, so each index of ctx receives exactly 4 blocks (index of ctx of a position: dest_block // 4). For every ordered pair of indices of ctx, at most 1 of the first index's blocks take positions on the second, and some pair has exactly 1. tile_list[p, 0] == p; the 4 tiles of a row are distinct and all on the same index of ctx as p (tile_list[p, j] // 4 == p // 4). Each stripe lies in the rows of one index of ctx: stripe_start // 512 == (stripe_start + 511) // 512 (since a stripe is 512 keys long, stripe_start is a multiple of 512).
All inputs are finite; a program needn't handle non-finite values.
Results may differ from a plain program's by a relative error of at most 0.0048.
Values may be sent and summed in bfloat16 or wider, within the bound.
No kernel may reach another device: no remote copies, remote signals or barrier semaphores. Data moves between devices by JAX's collectives and lax.ppermute only.
A program may use at most 64 MiB of HBM per device.

v0:
```python
import jax
import jax.numpy as jnp
from jax import lax
from jax.sharding import PartitionSpec as P

STRIPE = 512


def attend(query_block, tile_key, tile_value, tile_used, stripe_keys, stripe_values):
    scaling = query_block.shape[-1] ** (-0.5)
    block_rows = query_block.shape[0]
    near_scores = (
        jnp.einsum("qhgd,khd->hgqk", query_block, tile_key, preferred_element_type=jnp.float32)
        * scaling
    )
    far_scores = (
        jnp.einsum("qhgd,hkd->hgqk", query_block, stripe_keys, preferred_element_type=jnp.float32)
        * scaling
    )
    kept_mask = jnp.arange(near_scores.shape[-1], dtype=jnp.int32) // block_rows < tile_used
    near_scores = jnp.where(kept_mask, near_scores, -1e30)
    row_top = jnp.maximum(jnp.max(near_scores, axis=-1), jnp.max(far_scores, axis=-1))[..., None]
    near_weight = jnp.exp(near_scores - row_top)
    far_weight = jnp.exp(far_scores - row_top)
    denominator = jnp.sum(near_weight, axis=-1) + jnp.sum(far_weight, axis=-1)
    summed = jnp.einsum(
        "hgqk,khd->qhgd",
        near_weight.astype(jnp.bfloat16),
        tile_value,
        preferred_element_type=jnp.float32,
    )
    summed = summed + jnp.einsum(
        "hgqk,hkd->qhgd",
        far_weight.astype(jnp.bfloat16),
        stripe_values,
        preferred_element_type=jnp.float32,
    )
    return (summed / jnp.transpose(denominator, (2, 0, 1))[..., None]).astype(jnp.bfloat16)


def attend_all(
    query_blocks, tile_ids, counts, key_blocks, value_blocks, stripe_keys, stripe_values
):
    head_local = key_blocks.shape[2]
    head_width = key_blocks.shape[3]

    def attend_block(packed):
        query_block, tile_row, tile_used = packed
        tile_key = key_blocks[tile_row].reshape(-1, head_local, head_width)
        tile_value = value_blocks[tile_row].reshape(-1, head_local, head_width)
        return attend(query_block, tile_key, tile_value, tile_used, stripe_keys, stripe_values)

    return lax.map(attend_block, (query_blocks, tile_ids, counts))


def local(query_rows, key_rows, value_rows, dest_block, tile_list, tile_count, stripe_start):
    device_count = lax.axis_size("ctx")
    ctx_index = lax.axis_index("ctx")
    tok_rows, head_local, group_local, head_width = query_rows.shape
    block_total = dest_block.shape[0]
    per_device = block_total // device_count
    block_rows = tok_rows // per_device
    stripe_count = stripe_start.shape[1]
    capacity = max(1, per_device // device_count)
    block_index = jnp.arange(block_total, dtype=jnp.int32)
    inverse = jnp.zeros((block_total,), jnp.int32).at[dest_block].set(block_index)
    local_index = jnp.arange(per_device, dtype=jnp.int32)
    own_ids = ctx_index * per_device + local_index
    owner_dev = (dest_block // per_device).reshape(device_count, per_device)
    earlier = local_index[:, None] > local_index[None, :]
    same_dest = owner_dev[:, :, None] == owner_dev[:, None, :]
    rank_table = jnp.sum((same_dest & earlier[None]).astype(jnp.int32), axis=2)
    send_slots = owner_dev * capacity + rank_table
    own_slots = send_slots[ctx_index]
    slot_range = jnp.arange(device_count * capacity, dtype=jnp.int32)
    slot_source = jnp.sum(
        jnp.where(own_slots[:, None] == slot_range[None, :], local_index[:, None], 0), axis=0
    )
    query_flat = query_rows.reshape(per_device, block_rows, head_local * group_local * head_width)
    key_flat = key_rows.reshape(per_device, block_rows, head_local * head_width)
    value_flat = value_rows.reshape(per_device, block_rows, head_local * head_width)
    arrived = (
        lax.all_to_all(query_flat[slot_source], "ctx", split_axis=0, concat_axis=0, tiled=True),
        lax.all_to_all(key_flat[slot_source], "ctx", split_axis=0, concat_axis=0, tiled=True),
        lax.all_to_all(value_flat[slot_source], "ctx", split_axis=0, concat_axis=0, tiled=True),
    )
    anchor = inverse[own_ids]
    arrive_slot = (
        anchor // per_device * capacity + rank_table[anchor // per_device, anchor % per_device]
    )
    query_new = arrived[0][arrive_slot].reshape(
        per_device, block_rows, head_local, group_local, head_width
    )
    key_new = arrived[1][arrive_slot].reshape(tok_rows, head_local, head_width)
    value_new = arrived[2][arrive_slot].reshape(tok_rows, head_local, head_width)
    stripe_first = stripe_start.reshape(-1)
    stripe_head = jnp.arange(stripe_first.shape[0], dtype=jnp.int32) // stripe_count

    def cut_stripe(head_id, first_row):
        offset = first_row % tok_rows
        key_head = lax.dynamic_index_in_dim(key_new, head_id, 1, keepdims=False)
        value_head = lax.dynamic_index_in_dim(value_new, head_id, 1, keepdims=False)
        return jnp.stack([key_head, value_head])

    pieces = jax.vmap(cut_stripe)(stripe_head, stripe_first)
    owned = (stripe_first // tok_rows == ctx_index)[:, None, None, None]
    owned_terms = jnp.where(owned, pieces, jnp.zeros((), jnp.bfloat16))
    stacked = lax.psum(owned_terms, "ctx").astype(jnp.float32).astype(jnp.bfloat16)
    stripe_keys = stacked[:, 0].reshape(head_local, stripe_count * STRIPE, head_width)
    stripe_values = stacked[:, 1].reshape(head_local, stripe_count * STRIPE, head_width)
    tiles_new = tile_list[own_ids] - ctx_index * per_device
    counts = tile_count[own_ids]
    key_blocks = key_new.reshape(per_device, block_rows, head_local, head_width)
    value_blocks = value_new.reshape(per_device, block_rows, head_local, head_width)
    out_new = attend_all(
        query_new, tiles_new, counts, key_blocks, value_blocks, stripe_keys, stripe_values
    )
    return_source = jnp.sum(
        jnp.where(arrive_slot[:, None] == slot_range[None, :], local_index[:, None], 0), axis=0
    )
    returned = lax.all_to_all(
        out_new.reshape(per_device, block_rows, -1)[return_source],
        "ctx",
        split_axis=0,
        concat_axis=0,
        tiled=True,
    )
    result = returned[own_slots].reshape(query_rows.shape)
    return result


def solution(mesh):
    in_specs = (
        P(("parts", "ctx"), "head", "rep", None),
        P(("parts", "ctx"), "head", None),
        P(("parts", "ctx"), "head", None),
        P("parts"),
        P("parts", None),
        P("parts"),
        P(("parts", "head"), None),
    )
    out_specs = P(("parts", "ctx"), "head", "rep", None)
    return jax.shard_map(local, mesh=mesh, in_specs=in_specs, out_specs=out_specs, check_vma=False)
```

profile of v0, /device:TPU:1, one launch (start us, length us, event | category | flops | bytes accessed | tf_op | source)
XLA Modules:
  0.0 428.2 jit_solution(15590666713226647487)
XLA Ops:
  10.3 5.4 %all-to-all-start.1 = ((bf16[4,128,512]{2,1,0:T(8,128)(2,1)}), bf16[4,128,512]{2,1,0:T(8,128)(2,1)S(1)}, u32[]{:S(2)}, u32[]{:S(2)}) async-start(bf16[4,128,512]{2,1,0:T(8,128)(2,1)} %gather_fusion.8), calls=%async_computation.1 | async-start | bytes 1048576 | tf_op jit(solution)/shard_map/all_to_all | solution.py:84
  18.6 11.2 %all-to-all-done.1 = bf16[4,128,512]{2,1,0:T(8,128)(2,1)S(1)} async-done(((bf16[4,128,512]{2,1,0:T(8,128)(2,1)}), bf16[4,128,512]{2,1,0:T(8,128)(2,1)S(1)}, u32[]{:S(2)}, u32[]{:S(2)}) %all-to-all-start.1) | async-done | bytes 524320 | tf_op jit(solution)/shard_map/all_to_all | solution.py:84
  29.8 3.5 all-to-all-start
  36.0 11.3 %all-to-all-done = bf16[4,128,512]{2,1,0:T(8,128)(2,1)S(1)} async-done(((bf16[4,128,512]{2,1,0:T(8,128)(2,1)}), bf16[4,128,512]{2,1,0:T(8,128)(2,1)S(1)}, u32[]{:S(2)}, u32[]{:S(2)}) %all-to-all-start) | async-done | bytes 524320 | tf_op jit(solution)/shard_map/all_to_all | solution.py:85
  51.8 3.5 fusion.60
  60.4 3.8 gather_fusion.10
  64.2 3.9 all-to-all-start.2
  71.3 75.4 %all-to-all-done.2 = bf16[4,128,1536]{2,1,0:T(8,128)(2,1)S(1)} async-done(((bf16[4,128,1536]{2,1,0:T(8,128)(2,1)}), bf16[4,128,1536]{2,1,0:T(8,128)(2,1)S(1)}, u32[]{:S(2)}, u32[]{:S(2)}) %all-to-all-start.2) | async-done | bytes 1572896 | tf_op jit(solution)/shard_map/all_to_all | solution.py:83
  148.9 94.6 %all-reduce.2.cloned.1.call-done = bf16[16,2,512,128]{2,3,0,1:T(8,128)(2,1)} async-done(((bf16[16,2,512,128]{2,3,0,1:T(8,128)(2,1)}), bf16[16,2,512,128]{2,3,0,1:T(8,128)(2,1)}) %all-reduce.2.cloned.1.call-update) | async-done | bytes 4194320 | tf_op jit(solution)/shard_map/psum | solution.py:108
  243.6 3.9 fusion.80
  247.5 3.9 copy.85
  253.8 115.6 %while.12 = (s32[]{:T(128)}, bf16[4,128,4,3,128]{1,4,3,2,0:T(8,128)(2,1)}, s32[4,4]{1,0:T(4,128)S(1)}, bf16[4,128,4,128]{3,2,1,0:T(4,128)(2,1)}, s32[4]{0:T(128)...) while((s32[]{:T(128)}, ...), condition=%wide.region_9.10_spmd, body=%wide.region_4.9_spmd.sunk | while | flops 2047674880 | bytes 124487448 | solution.py:53
  268.8 8.0 %fusion.97 = f32[128,4,3,128]{0,3,2,1:T(8,128)} fusion(bf16[4,2048,128]{2,1,0:T(8,128)(2,1)S(1)} %copy-done.3, f32[4,128,3,2048]{3,1,2,0:T(8,128)} %copy-done.2, f32[4,3,128]{2,1,0:T(4,128)S(1)} %max.11), kind=kOutput, calls=%fused_computation.39.clone.1 | convolution fusion | flops 814743552 | bytes 15472640 | tf_op jit(solution)/shard_map/while/body/eval_jaxpr/hgqk,hkd->qhgd/dot_general | solution.py:32
  279.6 3.1 fusion.100
  288.6 3.0 bitcast_reduce_fusion.4
  297.7 8.0 %fusion.97 = f32[128,4,3,128]{0,3,2,1:T(8,128)} fusion(bf16[4,2048,128]{2,1,0:T(8,128)(2,1)S(1)} %copy-done.3, f32[4,128,3,2048]{3,1,2,0:T(8,128)} %copy-done.2, f32[4,3,128]{2,1,0:T(4,128)S(1)} %max.11), kind=kOutput, calls=%fused_computation.39.clone.1 | convolution fusion | flops 814743552 | bytes 15472640 | tf_op jit(solution)/shard_map/while/body/eval_jaxpr/hgqk,hkd->qhgd/dot_general | solution.py:32
  308.5 3.1 fusion.100
  326.6 8.0 %fusion.97 = f32[128,4,3,128]{0,3,2,1:T(8,128)} fusion(bf16[4,2048,128]{2,1,0:T(8,128)(2,1)S(1)} %copy-done.3, f32[4,128,3,2048]{3,1,2,0:T(8,128)} %copy-done.2, f32[4,3,128]{2,1,0:T(4,128)S(1)} %max.11), kind=kOutput, calls=%fused_computation.39.clone.1 | convolution fusion | flops 814743552 | bytes 15472640 | tf_op jit(solution)/shard_map/while/body/eval_jaxpr/hgqk,hkd->qhgd/dot_general | solution.py:32
  337.5 3.1 fusion.100
  355.5 8.0 %fusion.97 = f32[128,4,3,128]{0,3,2,1:T(8,128)} fusion(bf16[4,2048,128]{2,1,0:T(8,128)(2,1)S(1)} %copy-done.3, f32[4,128,3,2048]{3,1,2,0:T(8,128)} %copy-done.2, f32[4,3,128]{2,1,0:T(4,128)S(1)} %max.11), kind=kOutput, calls=%fused_computation.39.clone.1 | convolution fusion | flops 814743552 | bytes 15472640 | tf_op jit(solution)/shard_map/while/body/eval_jaxpr/hgqk,hkd->qhgd/dot_general | solution.py:32
  366.4 3.1 fusion.100
  372.9 3.6 all-to-all-start.3
  376.5 36.4 %all-to-all-done.3 = bf16[4,128,1536]{2,1,0:T(8,128)(2,1)S(1)} async-done(((bf16[4,128,1536]{2,1,0:T(8,128)(2,1)}), bf16[4,128,1536]{2,1,0:T(8,128)(2,1)S(1)}, u32[]{:S(2)}, u32[]{:S(2)}) %all-to-all-start.3) | async-done | bytes 1572896 | tf_op jit(solution)/shard_map/all_to_all | solution.py:121
  414.8 4.6 %reshape.508 = bf16[512,4,3,128]{3,2,1,0:T(4,128)(2,1)S(1)} reshape(bf16[4,128,1536]{2,1,0:T(8,128)(2,1)} %gather_fusion.15) | data formatting | bytes 3145728 | tf_op jit(solution)/shard_map/reshape | solution.py:128
  (146 shorter events, 102.1 us)
Async XLA Ops:
  6.5 62.2 %copy-start = (s32[16]{0:T(128)S(1)}, s32[16]{0:T(128)}, u32[]{:S(2)}) copy-start(s32[16]{0:T(128)} %param.14) | copy-start | bytes 196
  6.5 9.2 %copy-start.9 = (bf16[512,4,128]{2,1,0:T(4,128)(2,1)S(1)}, bf16[512,4,128]{2,1,0:T(4,128)(2,1)}, u32[]{:S(2)}) copy-start(bf16[512,4,128]{2,1,0:T(4,128)(2,1)} %param.11) | copy-start | bytes 1572868
  10.3 19.5 %all-to-all-start.1 = ((bf16[4,128,512]{2,1,0:T(8,128)(2,1)}), bf16[4,128,512]{2,1,0:T(8,128)(2,1)S(1)}, u32[]{:S(2)}, u32[]{:S(2)}) async-start(bf16[4,128,512]{2,1,0:T(8,128)(2,1)} %gather_fusion.8), calls=%async_computation.1 | async-start | bytes 1048576 | tf_op jit(solution)/shard_map/all_to_all | solution.py:84
  15.7 18.2 %copy-start.11 = (s32[4,4]{1,0:T(4,128)S(1)}, s32[4,4]{1,0:T(4,128)}, u32[]{:S(2)}) copy-start(s32[4,4]{1,0:T(4,128)} %param.15) | copy-start | bytes 196
  29.8 17.5 %all-to-all-start = ((bf16[4,128,512]{2,1,0:T(8,128)(2,1)}), bf16[4,128,512]{2,1,0:T(8,128)(2,1)S(1)}, u32[]{:S(2)}, u32[]{:S(2)}) async-start(bf16[4,128,512]{2,1,0:T(8,128)(2,1)} %gather_fusion.3), calls=%async_computation | async-start | bytes 1048576 | tf_op jit(solution)/shard_map/all_to_all | solution.py:85
  33.3 210.3 %all-reduce.2.cloned.1.call-start = ((), (), s32[]{:S(2)}) async-start(), calls=%async_computation.4 | async-start | bytes 8388608 | tf_op jit(solution)/shard_map/psum | solution.py:108
  64.2 3.9 copy-start.10
  64.2 5.3 %copy-start.8 = (bf16[4,128,512]{2,1,0:T(8,128)(2,1)S(1)}, bf16[4,128,512]{2,1,0:T(8,128)(2,1)}, u32[]{:S(2)}) copy-start(bf16[4,128,512]{2,1,0:T(8,128)(2,1)} %copy-done.7) | copy-start | bytes 1572868
  64.2 6.3 %copy-start.6 = (bf16[4,128,512]{2,1,0:T(8,128)(2,1)S(1)}, bf16[4,128,512]{2,1,0:T(8,128)(2,1)}, u32[]{:S(2)}) copy-start(bf16[4,128,512]{2,1,0:T(8,128)(2,1)} %copy-done.5) | copy-start | bytes 1572868
  64.2 82.5 %all-to-all-start.2 = ((bf16[4,128,1536]{2,1,0:T(8,128)(2,1)}), bf16[4,128,1536]{2,1,0:T(8,128)(2,1)S(1)}, u32[]{:S(2)}, u32[]{:S(2)}) async-start(bf16[4,128,1536]{2,1,0:T(8,128)(2,1)} %gather_fusion.10), calls=%async_computation.2 | async-start | bytes 3145728 | tf_op jit(solution)/shard_map/all_to_all | solution.py:83
  256.6 3.1 copy-start.4
  262.7 4.6 %copy-start.2 = (f32[4,128,3,2048]{3,1,2,0:T(8,128)}, f32[4,128,3,2048]{3,1,2,0:T(8,128)S(1)}, u32[]{:S(2)}) copy-start(f32[4,128,3,2048]{3,1,2,0:T(8,128)S(1)} %get-tuple-element.250) | copy-start | bytes 37748740 | tf_op jit(solution)/shard_map/while
  267.2 1.6 copy-start.3
  285.5 3.1 copy-start.4
  291.6 4.6 %copy-start.2 = (f32[4,128,3,2048]{3,1,2,0:T(8,128)}, f32[4,128,3,2048]{3,1,2,0:T(8,128)S(1)}, u32[]{:S(2)}) copy-start(f32[4,128,3,2048]{3,1,2,0:T(8,128)S(1)} %get-tuple-element.250) | copy-start | bytes 37748740 | tf_op jit(solution)/shard_map/while
  296.1 1.6 copy-start.3
  314.4 3.1 copy-start.4
  320.5 4.6 %copy-start.2 = (f32[4,128,3,2048]{3,1,2,0:T(8,128)}, f32[4,128,3,2048]{3,1,2,0:T(8,128)S(1)}, u32[]{:S(2)}) copy-start(f32[4,128,3,2048]{3,1,2,0:T(8,128)S(1)} %get-tuple-element.250) | copy-start | bytes 37748740 | tf_op jit(solution)/shard_map/while
  325.0 1.6 copy-start.3
  343.3 3.1 copy-start.4
  349.4 4.6 %copy-start.2 = (f32[4,128,3,2048]{3,1,2,0:T(8,128)}, f32[4,128,3,2048]{3,1,2,0:T(8,128)S(1)}, u32[]{:S(2)}) copy-start(f32[4,128,3,2048]{3,1,2,0:T(8,128)S(1)} %get-tuple-element.250) | copy-start | bytes 37748740 | tf_op jit(solution)/shard_map/while
  353.9 1.6 copy-start.3
  372.9 40.1 %all-to-all-start.3 = ((bf16[4,128,1536]{2,1,0:T(8,128)(2,1)}), bf16[4,128,1536]{2,1,0:T(8,128)(2,1)S(1)}, u32[]{:S(2)}, u32[]{:S(2)}) async-start(bf16[4,128,1536]{2,1,0:T(8,128)(2,1)} %gather_fusion.14), calls=%async_computation.3 | async-start | bytes 3145728 | tf_op jit(solution)/shard_map/all_to_all | solution.py:121
  414.8 6.6 %copy-start.1 = (s32[16]{0:T(128)S(1)}, s32[16]{0:T(128)}, u32[]{:S(2)}) copy-start(s32[16]{0:T(128)} %param.14) | copy-start | bytes 196
  (2 other events, 1.6 us)
Sparse Core Ops, SparseCore 0:
  55.5 188.0 all-reduce.1
where the time goes:
time: 431 us; the launch traced here: 428 us
  waiting for transfers between devices  229 us (53%)
  local copies, waits for them, and re-layouts  85.3 us (20%)
  matrix products  63.5 us (15%)
  other arithmetic  20.2 us (5%)
  starting transfers between devices  16.4 us (4%)
  between operations  13.7 us (3%)
    psum x1, waiting for transfers between devices, local(): lax.psum(owned_terms, 'ctx').astype(jnp.float32).astype(jnp.bfloat16)  94.6 us
    all_to_all x1, waiting for transfers between devices, local(): lax.all_to_all(query_flat[slot_source], 'ctx', split_axis=0, concat_axis=...  75.4 us
    all_to_all x1, waiting for transfers between devices, local(): lax.all_to_all(out_new.reshape(per_device, block_rows, -1)[return_source]...  36.4 us
    dot_general x4, matrix products, attend(): jnp.einsum('hgqk,hkd->qhgd', far_weight.astype(jnp.bfloat16), stripe_valu...  32.1 us
    reduce_sum x8, other arithmetic, attend(): denominator = jnp.sum(near_weight, axis=-1) + jnp.sum(far_weight, axis=-1)  12.7 us
    dot_general x4, matrix products, attend(): jnp.einsum('hgqk,khd->qhgd', near_weight.astype(jnp.bfloat16), tile_value...  12.2 us
    dot_general x4, matrix products, attend(): jnp.einsum('qhgd,hkd->hgqk', query_block, stripe_keys, preferred_element_...  12 us
    while x24, local copies, waits for them, and re-layouts  11.8 us
  transfers between devices with their start and end apart: 5, of which 5 were waited for; matrix products, arithmetic and copies ran while one was open for 4% of the time, Pallas kernels for 0%

commit v1 on v0

v1 whole, which is shorter than its diff:
```python
import functools
import math

import jax
import jax.numpy as jnp
from jax import lax
from jax.experimental import pallas as pl
from jax.experimental.pallas import tpu as pltpu
from jax.sharding import PartitionSpec as P

NEG = -1e30


def attend_kernel(slots, first, last, scale, *refs):
    src_ref, bias_ref, q_ref = refs[:3]
    kv_refs = refs[3 : 3 + 2 * slots]
    rest = refs[3 + 2 * slots :]
    if first:
        acc_in, top_in = None, None
        outs = rest
    else:
        acc_in, top_in = rest[:2]
        outs = rest[2:]
    pairs, rows, width = q_ref.shape
    heads = kv_refs[0].shape[1]
    half = kv_refs[0].shape[2]
    blocks = pairs // heads
    block_rows = half * 2 // blocks
    half_blocks = half // block_rows
    rep = src_ref[0]
    ones = jnp.ones((half, width), jnp.bfloat16)

    def update(pair, slot, acc_src, top_src, acc_dst, top_dst, fresh):
        head = pair // blocks
        source = src_ref[1 + slot]
        query = q_ref[pair]
        scores = []
        for part in range(2):
            ref = kv_refs[2 * slot + part]
            raw = lax.dot_general(
                query, ref[0, head], (((1,), (1,)), ((), ())), preferred_element_type=jnp.float32
            )
            base = source * blocks + (rep if part == 0 else 1 - rep) * half_blocks
            for piece in range(half_blocks):
                cut = raw[:, piece * block_rows : (piece + 1) * block_rows]
                scores.append(cut * scale + bias_ref[pair, base + piece])
        top = functools.reduce(jnp.maximum, scores)
        top = jnp.max(top, axis=-1, keepdims=True)
        if not fresh:
            before = top_src[pair][:, :1]
            top = jnp.maximum(top, before)
        weights = [jnp.exp2(piece - top).astype(jnp.bfloat16) for piece in scores]
        total = None
        for part in range(2):
            ref = kv_refs[2 * slot + part]
            value = jnp.concatenate([ref[1, head], ones], axis=1)
            weight = jnp.concatenate(
                weights[part * half_blocks : (part + 1) * half_blocks], axis=1
            )
            term = jnp.dot(weight, value, preferred_element_type=jnp.float32)
            total = term if total is None else total + term
        if not fresh:
            total = total + acc_src[pair] * jnp.exp2(before - top)
        acc_dst[pair] = total
        top_dst[pair] = jnp.broadcast_to(top, top_dst.shape[1:])

    if first:
        acc_dst, top_dst = outs[:2]
    elif last:
        acc_dst, top_dst = outs[1:3]
    else:
        acc_dst, top_dst = outs[:2]

    if first:
        @pl.loop(0, pairs)
        def _(pair):
            update(pair, 0, None, None, acc_dst, top_dst, True)
    else:

        @pl.loop(0, pairs)
        def _(pair):
            acc_dst[pair] = acc_in[pair]
            top_dst[pair] = top_in[pair]

        for slot in range(slots):

            @pl.when(src_ref[1 + slot] >= 0)
            def _():
                @pl.loop(0, pairs)
                def _(pair):
                    update(pair, slot, acc_dst, top_dst, acc_dst, top_dst, False)
    if last:
        out_ref = outs[0]

        @pl.loop(0, pairs)
        def _(pair):
            total = acc_dst[pair]
            out_ref[pair] = (total[:, :width] / total[:, width:]).astype(out_ref.dtype)


def attend_call(sources, bias, query, kv, state, last, scale):
    pairs, rows, width = query.shape
    slots = len(kv) // 2
    first = state is None
    vmem = pl.BlockSpec(memory_space=pltpu.VMEM)
    smem = pl.BlockSpec(memory_space=pltpu.SMEM)
    operands = [sources, bias, query, *kv]
    specs = [smem, smem] + [vmem] * (1 + len(kv))
    shapes = [
        jax.ShapeDtypeStruct((pairs, rows, 2 * width), jnp.float32),
        jax.ShapeDtypeStruct((pairs, rows, width), jnp.float32),
    ]
    aliases = {}
    if not first:
        aliases = {len(operands): 0, len(operands) + 1: 1}
        operands += list(state)
        specs += [vmem, vmem]
    if last:
        shapes = [jax.ShapeDtypeStruct((pairs, rows, width), jnp.bfloat16)] + shapes
        aliases = {key: value + 1 for key, value in aliases.items()}
    keys = slots * 2 * kv[0].shape[2]
    work = pairs * rows * keys
    return pl.pallas_call(
        functools.partial(attend_kernel, slots, first, last, scale),
        out_shape=shapes,
        in_specs=specs,
        out_specs=[vmem] * len(shapes),
        input_output_aliases=aliases,
        compiler_params=pltpu.CompilerParams(vmem_limit_bytes=40 << 20),
        cost_estimate=pl.CostEstimate(
            flops=6 * work * width, bytes_accessed=4 * pairs * rows * width, transcendentals=work
        ),
    )(*operands)


def local(query_rows, key_rows, value_rows, dest_block, tile_list, tile_count, stripe_start):
    ctx_count = lax.axis_size("ctx")
    ctx_index = lax.axis_index("ctx")
    rep_index = lax.axis_index("rep")
    tok_rows, heads, group, width = query_rows.shape
    block_total = dest_block.shape[0]
    blocks = block_total // ctx_count
    block_rows = tok_rows // blocks
    half = tok_rows // 2
    scale = width ** (-0.5) * math.log2(math.e)

    def half_of(which):
        key_half = lax.dynamic_slice_in_dim(key_rows, which * half, half, 0)
        value_half = lax.dynamic_slice_in_dim(value_rows, which * half, half, 0)
        return jnp.transpose(jnp.stack([key_half, value_half]), (0, 2, 1, 3))

    def swap(array):
        return lax.ppermute(array, "rep", [(0, 1), (1, 0)])

    mine = half_of(rep_index)
    right = [(i, i + 1) for i in range(ctx_count - 1)]
    left = [(i + 1, i) for i in range(ctx_count - 1)]
    steps = []
    from_left, from_right = mine, mine
    for hop in range(1, max(2, ctx_count - 1)):
        if ctx_count == 1:
            break
        from_left = lax.ppermute(from_left, "ctx", right)
        from_right = lax.ppermute(from_right, "ctx", left)
        steps.append(
            (
                (from_left, from_right),
                (ctx_index - hop, jnp.where(ctx_index + hop < ctx_count, ctx_index + hop, -1)),
            )
        )
        if hop == 1 and ctx_count > 2:
            far = lax.ppermute(mine, "ctx", [(0, ctx_count - 1), (ctx_count - 1, 0)])
            far_source = jnp.where(
                ctx_index == 0, ctx_count - 1, jnp.where(ctx_index == ctx_count - 1, 0, -1)
            )
            steps.append(((far,), (far_source,)))

    owner = dest_block // blocks
    stripes = jnp.sum(
        (stripe_start[:, :, None] // tok_rows == owner[None, None, :]).astype(jnp.int32), axis=1
    )
    placed = lax.dynamic_slice_in_dim(dest_block, ctx_index * blocks, blocks, 0)
    row_pick = (placed[:, None] == jnp.arange(block_total)[None, :]).astype(jnp.int32)
    used = jnp.arange(tile_list.shape[1])[None, :] < tile_count[:, None]
    listed = jnp.sum(
        (used[:, :, None] & (tile_list[:, :, None] == dest_block[None, None, :])).astype(jnp.int32),
        axis=1,
    )
    near = jnp.sum(row_pick[:, :, None] * listed[None], axis=1)
    count = stripes[:, None, :] + near[None, :, :]
    bias = jnp.where(count > 0, jnp.log2(jnp.maximum(count, 1).astype(jnp.float32)), NEG)
    bias = bias.reshape(heads * blocks, block_total)

    query = query_rows.reshape(blocks, block_rows, heads, group, width)
    query = jnp.transpose(query, (2, 0, 3, 1, 4)).reshape(
        heads * blocks, group * block_rows, width
    )

    def scalars(values):
        return jnp.stack([rep_index, *values]).astype(jnp.int32)

    state = attend_call(
        scalars((ctx_index,)),
        bias,
        query,
        (mine, half_of(1 - rep_index)),
        None,
        False,
        scale,
    )
    if not steps:
        total = state[0]
        out = (total[..., :width] / total[..., width:]).astype(jnp.bfloat16)
    for index, (arrays, sources) in enumerate(steps):
        kv = []
        for array in arrays:
            kv += [array, swap(array)]
        last = index == len(steps) - 1
        state = attend_call(scalars(sources), bias, query, kv, state, last, scale)
        if last:
            out = state[0]
    out = out.reshape(heads, blocks, group, block_rows, width)
    return jnp.transpose(out, (1, 3, 0, 2, 4)).reshape(query_rows.shape)


def solution(mesh):
    in_specs = (
        P(("parts", "ctx"), "head", "rep", None),
        P(("parts", "ctx"), "head", None),
        P(("parts", "ctx"), "head", None),
        P("parts"),
        P("parts", None),
        P("parts"),
        P(("parts", "head"), None),
    )
    out_specs = P(("parts", "ctx"), "head", "rep", None)
    return jax.shard_map(local, mesh=mesh, in_specs=in_specs, out_specs=out_specs, check_vma=False)
```

time: 431 us -> 113 us (0.26)
  waiting for transfers between devices: 229 us -> 9.95 us
  local copies, waits for them, and re-layouts: 85.3 us -> 12.9 us
  Pallas kernels: 0 us -> 66.2 us
  matrix products: 63.5 us -> 0 us
  other arithmetic: 20.2 us -> 1.73 us
  between operations: 13.7 us -> 0.22 us
  starting transfers between devices: 16.4 us -> 21.3 us
    all_to_all x4 -> x0, waiting for transfers between devices: 134 us -> none  [the longest x1 75.4 us: local(): lax.all_to_all(query_flat[slot_source], 'ctx', split_axis=0, concat_axis=...]
    psum x1 -> x0, waiting for transfers between devices: 94.6 us -> none  [local(): lax.psum(owned_terms, 'ctx').astype(jnp.float32).astype(jnp.bfloat16)]
    pallas_call x0 -> x4, Pallas kernels: none -> 66.2 us  [attend_call(): pl.pallas_call(functools.partial(attend_kernel, slots, first, last, scale...]
    dot_general x16 -> x0, matrix products: 63.5 us -> none  [the longest x4 32.1 us: attend(): jnp.einsum('hgqk,hkd->qhgd', far_weight.astype(jnp.bfloat16), stripe_valu...]
    gather x23 -> x0, local copies, waits for them, and re-layouts: 41.1 us -> none  [the longest x4 11.2 us: attend_block(): tile_key = key_blocks[tile_row].reshape(-1, head_local, head_width)]
    ppermute x0 -> x10, starting transfers between devices: none -> 21.3 us  [the longest x2 7.48 us: local(): from_left = lax.ppermute(from_left, 'ctx', right)]
    all_to_all x4 -> x0, starting transfers between devices: 16.3 us -> none  [the longest x1 5.41 us: local(): lax.all_to_all(key_flat[slot_source], 'ctx', split_axis=0, concat_axis=0,...]
    reshape x13 -> x1, local copies, waits for them, and re-layouts: 15.8 us -> 1.79 us  [local(): query = query_rows.reshape(blocks, block_rows, heads, group, width)]
  transfers between devices with their start and end apart: 5 -> 10, of which waited for: 5 -> 2; matrix products, arithmetic and copies ran while one was open for 4% -> 4% of each run, Pallas kernels for 0% -> 40%
where the time goes in v1:
time: 113 us; the launch traced here: 112 us
  Pallas kernels  66.2 us (59%)
  starting transfers between devices  21.3 us (19%)
  local copies, waits for them, and re-layouts  12.9 us (11%)
  waiting for transfers between devices  9.95 us (9%)
  other arithmetic  1.73 us (2%)
    pallas_call x4, Pallas kernels, attend_call(): pl.pallas_call(functools.partial(attend_kernel, slots, first, last, scale...  66.2 us
    ppermute x2, waiting for transfers between devices, local(): from_right = lax.ppermute(from_right, 'ctx', left)  7.58 us
    ppermute x2, starting transfers between devices, local(): from_left = lax.ppermute(from_left, 'ctx', right)  7.48 us
    ppermute x1, starting transfers between devices, local(): far = lax.ppermute(mine, 'ctx', [(0, ctx_count - 1), (ctx_count - 1, 0)])  6.77 us
    unnamed x14, local copies, waits for them, and re-layouts  6.27 us
    ppermute x5, starting transfers between devices, swap(): return lax.ppermute(array, 'rep', [(0, 1), (1, 0)])  4.51 us
    ppermute x2, starting transfers between devices, local(): from_right = lax.ppermute(from_right, 'ctx', left)  2.57 us
    transpose x1, local copies, waits for them, and re-layouts, local(): return jnp.transpose(out, (1, 3, 0, 2, 4)).reshape(query_rows.shape)  2.36 us
  transfers between devices with their start and end apart: 10, of which 2 were waited for; matrix products, arithmetic and copies ran while one was open for 4% of the time, Pallas kernels for 40%

profile of v1, /device:TPU:1, one launch (start us, length us, event | category | flops | bytes accessed | tf_op | source)
XLA Modules:
  0.0 112.4 jit_solution(11988823421884518964)
XLA Ops:
  0.0 1.6 %constant_dynamic-slice_fusion = (bf16[256,4,128]{2,1,0:T(4,128)(2,1)S(1)}, bf16[256,4,128]{2,1,0:T(4,128)(2,1)S(1)}, bf16[256,4,128]{2,1,0:T(4,128)(2,1)S(1)}, bf16[256,4,128]{2,1,0:T(4,128)(2,1)S(1)}) fusion(bf16[512,4,128]{2,1,0:T(4,128)(2,1)} %param.9, s32[]{:T(128)S(6)} %select_n.51, s32[]{:T(128)S(6)} %select_n.47, bf16[512,4,128]{2,1,0:T(4,128)(2,1)} %param.8), kind=kLoop, calls=%fused_computation.29 | loop fusion | bytes 2097160 | tf_op jit(solution)/shard_map/dynamic_slice | solution.py:149
  1.8 4.1 %collective-permute-start = (bf16[2,4,256,128]{3,2,1,0:T(8,128)(2,1)S(1)}, bf16[2,4,256,128]{3,2,1,0:T(8,128)(2,1)S(1)}, u32[]{:S(2)}, u32[]{:S(2)}) collective-permute-start(bf16[2,4,256,128]{3,2,1,0:T(8,128)(2,1)S(1)} %maximum_bitcast_fusion.refs_3_), channel_id=1, source_target_pairs={{0,4},{4,8},{8,12},{1,5},{5,9},{9,13},{2,6},{6,10},{10,14},{3,7},{... | collective-permute-start | bytes 1572872 | tf_op jit(solution)/shard_map/ppermute | solution.py:163
  5.8 1.3 %collective-permute-start.3 = (bf16[2,4,256,128]{3,2,1,0:T(8,128)(2,1)S(1)}, bf16[2,4,256,128]{3,2,1,0:T(8,128)(2,1)}, u32[]{:S(2)}, u32[]{:S(2)}) collective-permute-start(bf16[2,4,256,128]{3,2,1,0:T(8,128)(2,1)S(1)} %maximum_bitcast_fusion.refs_3_), channel_id=1, source_target_pairs={{4,0},{8,4},{12,8},{5,1},{9,5},{13,9},{6,2},{10,6},{14,10},{7,3},{... | collective-permute-start | bytes 1572872 | tf_op jit(solution)/shard_map/ppermute | solution.py:164
  7.1 6.8 %collective-permute-start.6 = (bf16[2,4,256,128]{3,2,1,0:T(8,128)(2,1)S(1)}, bf16[2,4,256,128]{3,2,1,0:T(8,128)(2,1)S(1)}, u32[]{:S(2)}, u32[]{:S(2)}) collective-permute-start(bf16[2,4,256,128]{3,2,1,0:T(8,128)(2,1)S(1)} %maximum_bitcast_fusion.refs_3_), channel_id=1, source_target_pairs={{0,12},{12,0},{1,13},{13,1},{2,14},{14,2},{3,15},{15,3},{16,28},{2... | collective-permute-start | bytes 1572872 | tf_op jit(solution)/shard_map/ppermute | solution.py:172
  13.9 0.7 copy.32
  14.8 1.8 %copy.21 = bf16[4,128,4,3,128]{4,1,3,0,2:T(8,128)(2,1)S(1)} copy(bf16[4,128,4,3,128]{4,2,3,1,0:T(4,128)(2,1)} %bitcast.41) | data formatting | bytes 3145728 | tf_op jit(solution)/shard_map/reshape | solution.py:194
  17.1 1.0 maximum_bitcast_fusion.1.refs_4_
  18.2 1.5 %collective-permute-start.8 = (bf16[2,4,256,128]{3,2,1,0:T(8,128)(2,1)S(1)}, bf16[2,4,256,128]{3,2,1,0:T(8,128)(2,1)S(1)}, u32[]{:S(2)}, u32[]{:S(2)}) collective-permute-start(bf16[2,4,256,128]{3,2,1,0:T(8,128)(2,1)S(1)} %collective-permute-done.refs_3_), channel_id=1, source_target_pairs={{0,1},{1,0},{2,3},{3,2},{4,5},{5,4},{6,7},{7,6},{8,9},{9,8},{10,11... | collective-permute-start | bytes 1572872 | tf_op jit(solution)/shard_map/ppermute | solution.py:153
  19.7 3.4 %collective-permute-start.1 = (bf16[2,4,256,128]{3,2,1,0:T(8,128)(2,1)S(1)}, bf16[2,4,256,128]{3,2,1,0:T(8,128)(2,1)S(1)}, u32[]{:S(2)}, u32[]{:S(2)}) collective-permute-start(bf16[2,4,256,128]{3,2,1,0:T(8,128)(2,1)S(1)} %collective-permute-done.refs_3_), channel_id=1, source_target_pairs={{0,4},{4,8},{8,12},{1,5},{5,9},{9,13},{2,6},{6,10},{10,14},{3,7},{... | collective-permute-start | bytes 1572872 | tf_op jit(solution)/shard_map/ppermute | solution.py:163
  23.2 0.3 collective-permute-start.9
  23.5 1.3 %collective-permute-start.4 = (bf16[2,4,256,128]{3,2,1,0:T(8,128)(2,1)}, bf16[2,4,256,128]{3,2,1,0:T(8,128)(2,1)S(1)}, u32[]{:S(2)}, u32[]{:S(2)}) collective-permute-start(bf16[2,4,256,128]{3,2,1,0:T(8,128)(2,1)} %collective-permute-done.3.refs_5_), channel_id=1, source_target_pairs={{4,0},{8,4},{12,8},{5,1},{9,5},{13,9},{6,2},{10,6},{14,10},{7,3},{... | collective-permute-start | bytes 1572872 | tf_op jit(solution)/shard_map/ppermute | solution.py:164
  24.8 11.3 %shard_map.73 = (f32[16,384,256]{2,1,0:T(8,128)S(1)}, f32[16,384,128]{2,1,0:T(8,128)S(1)}) custom-call(s32[2]{0:T(128)S(1)} %pad_add_fusion.3.refs_0_, f32[16,16]{1,0:T(8,128)S(1)} %bitcast.37, bf16[16,384,128]{2,1,0:T(8,128)(2,1)S(1)} %bitcast.32, bf16[2,4,256,128]{3,2,1,0:T(8,128)(2,1)S(1)} %maximum_bitcast_fusion.refs_3_, ...), custom_call_target="tpu_custom_call" | custom-call | flops 2415919104 | bytes 3145728 | tf_op jit(solution)/shard_map/pallas_call | solution.py:123
  36.2 0.3 collective-permute-start.7
  36.5 2.4 %collective-permute-done.1.refs_3_ = bf16[2,4,256,128]{3,2,1,0:T(8,128)(2,1)S(1)} collective-permute-done((bf16[2,4,256,128]{3,2,1,0:T(8,128)(2,1)S(1)}, bf16[2,4,256,128]{3,2,1,0:T(8,128)(2,1)S(1)}, u32[]{:S(2)}, u32[]{:S(2)}) %collective-permute-start.1) | collective-permute-done | bytes 524320 | tf_op jit(solution)/shard_map/ppermute | solution.py:163
  38.9 1.5 %collective-permute-start.2 = (bf16[2,4,256,128]{3,2,1,0:T(8,128)(2,1)S(1)}, bf16[2,4,256,128]{3,2,1,0:T(8,128)(2,1)S(1)}, u32[]{:S(2)}, u32[]{:S(2)}) collective-permute-start(bf16[2,4,256,128]{3,2,1,0:T(8,128)(2,1)S(1)} %collective-permute-done.1.refs_3_), channel_id=1, source_target_pairs={{0,1},{1,0},{2,3},{3,2},{4,5},{5,4},{6,7},{7,6},{8,9},{9,8},{10,11... | collective-permute-start | bytes 1572872 | tf_op jit(solution)/shard_map/ppermute | solution.py:153
  40.4 7.6 %collective-permute-done.4.refs_5_ = bf16[2,4,256,128]{3,2,1,0:T(8,128)(2,1)S(1)} collective-permute-done((bf16[2,4,256,128]{3,2,1,0:T(8,128)(2,1)}, bf16[2,4,256,128]{3,2,1,0:T(8,128)(2,1)S(1)}, u32[]{:S(2)}, u32[]{:S(2)}) %collective-permute-start.4) | collective-permute-done | bytes 524320 | tf_op jit(solution)/shard_map/ppermute | solution.py:164
  48.0 0.8 collective-permute-start.5
  48.8 16.8 %shard_map.74 = (f32[16,384,256]{2,1,0:T(8,128)S(1)}, f32[16,384,128]{2,1,0:T(8,128)S(1)}) custom-call(s32[3]{0:T(128)S(1)} %pad_add_fusion.2.refs_0_, f32[16,16]{1,0:T(8,128)S(1)} %bitcast.38, bf16[16,384,128]{2,1,0:T(8,128)(2,1)S(1)} %bitcast.33, ...), custom_call_target="tpu_custom_call", output_to_operand_aliasing={{0}: (7, {}), {1}: (8, {})} | custom-call | flops 4831838208 | bytes 3145728 | tf_op jit(solution)/shard_map/pallas_call | solution.py:123
  65.7 16.5 %shard_map.75 = (f32[16,384,256]{2,1,0:T(8,128)S(1)}, f32[16,384,128]{2,1,0:T(8,128)S(1)}) custom-call(s32[2]{0:T(128)S(1)} %pad_add_fusion.1.refs_0_, f32[16,16]{1,0:T(8,128)S(1)} %bitcast.39, bf16[16,384,128]{2,1,0:T(8,128)(2,1)S(1)} %bitcast.34, ...), custom_call_target="tpu_custom_call", output_to_operand_aliasing={{0}: (5, {}), {1}: (6, {})} | custom-call | flops 2415919104 | bytes 3145728 | tf_op jit(solution)/shard_map/pallas_call | solution.py:123
  82.2 2.6 %copy-done = f32[16,384,256]{2,1,0:T(8,128)} copy-done((f32[16,384,256]{2,1,0:T(8,128)}, f32[16,384,256]{2,1,0:T(8,128)S(1)}, u32[]{:S(2)}) %copy-start) | copy-done | bytes 6291480
  84.8 1.7 %copy-done.1 = f32[16,384,128]{2,1,0:T(8,128)} copy-done((f32[16,384,128]{2,1,0:T(8,128)}, f32[16,384,128]{2,1,0:T(8,128)S(1)}, u32[]{:S(2)}) %copy-start.1) | copy-done | bytes 3145752
  86.5 1.9 %copy-done.2 = f32[16,384,128]{2,1,0:T(8,128)S(1)} copy-done((f32[16,384,128]{2,1,0:T(8,128)S(1)}, f32[16,384,128]{2,1,0:T(8,128)}, u32[]{:S(2)}) %copy-start.2) | copy-done | bytes 3145752
  88.4 21.6 %shard_map.76 = (bf16[16,384,128]{2,1,0:T(8,128)(2,1)S(1)}, f32[16,384,256]{2,1,0:T(8,128)}, f32[16,384,128]{2,1,0:T(8,128)S(1)}) custom-call(s32[3]{0:T(128)S(1)} %pad_add_fusion.refs_0_, f32[16,16]{1,0:T(8,128)S(1)} %bitcast.40, bf16[16,384,128]{2,1,0:T(8,128)(2,1)S(1)} %bitcast.35, ...), custom_call_target="tpu_custom_call", output_to_operand_aliasing={{1}: (7, {}), {2}: (8, {})} | custom-call | flops 4831838208 | bytes 3145728 | tf_op jit(solution)/shard_map/pallas_call | solution.py:123
  110.0 2.4 %copy.26 = bf16[4,128,4,3,128]{4,2,3,1,0:T(4,128)(2,1)} copy(bf16[4,128,4,3,128]{4,1,3,0,2:T(8,128)(2,1)S(1)} %bitcast.36) | data formatting | bytes 3145728 | tf_op jit(solution)/shard_map/transpose | solution.py:223
  (36 shorter events, 1.0 us)
Async XLA Ops:
  0.0 14.7 %copy-start.5 = (s32[16]{0:T(128)S(1)}, s32[16]{0:T(128)}, u32[]{:S(2)}) copy-start(s32[16]{0:T(128)} %param.10) | copy-start | bytes 196
  0.0 14.8 %copy-start.6 = (s32[16]{0:T(128)S(1)}, s32[16]{0:T(128)}, u32[]{:S(2)}) copy-start(s32[16]{0:T(128)} %param.12) | copy-start | bytes 196
  0.0 14.8 %copy-start.3 = (s32[4,4]{1,0:T(4,128)S(1)}, s32[4,4]{1,0:T(4,128)}, u32[]{:S(2)}) copy-start(s32[4,4]{1,0:T(4,128)} %param.13) | copy-start | bytes 196
  1.6 15.2 %copy-start.4 = (s32[16,4]{0,1:T(4,128)S(1)}, s32[16,4]{0,1:T(4,128)}, u32[]{:S(2)}) copy-start(s32[16,4]{0,1:T(4,128)} %param.11) | copy-start | bytes 772
  1.8 16.4 %collective-permute-start = (bf16[2,4,256,128]{3,2,1,0:T(8,128)(2,1)S(1)}, bf16[2,4,256,128]{3,2,1,0:T(8,128)(2,1)S(1)}, u32[]{:S(2)}, u32[]{:S(2)}) collective-permute-start(bf16[2,4,256,128]{3,2,1,0:T(8,128)(2,1)S(1)} %maximum_bitcast_fusion.refs_3_), channel_id=1, source_target_pairs={{0,4},{4,8},{8,12},{1,5},{5,9},{9,13},{2,6},{6,10},{10,14},{3,7},{... | collective-permute-start | bytes 1572872 | tf_op jit(solution)/shard_map/ppermute | solution.py:163
  5.8 17.4 %collective-permute-start.3 = (bf16[2,4,256,128]{3,2,1,0:T(8,128)(2,1)S(1)}, bf16[2,4,256,128]{3,2,1,0:T(8,128)(2,1)}, u32[]{:S(2)}, u32[]{:S(2)}) collective-permute-start(bf16[2,4,256,128]{3,2,1,0:T(8,128)(2,1)S(1)} %maximum_bitcast_fusion.refs_3_), channel_id=1, source_target_pairs={{4,0},{8,4},{12,8},{5,1},{9,5},{13,9},{6,2},{10,6},{14,10},{7,3},{... | collective-permute-start | bytes 1572872 | tf_op jit(solution)/shard_map/ppermute | solution.py:164
  7.1 29.0 %collective-permute-start.6 = (bf16[2,4,256,128]{3,2,1,0:T(8,128)(2,1)S(1)}, bf16[2,4,256,128]{3,2,1,0:T(8,128)(2,1)S(1)}, u32[]{:S(2)}, u32[]{:S(2)}) collective-permute-start(bf16[2,4,256,128]{3,2,1,0:T(8,128)(2,1)S(1)} %maximum_bitcast_fusion.refs_3_), channel_id=1, source_target_pairs={{0,12},{12,0},{1,13},{13,1},{2,14},{14,2},{3,15},{15,3},{16,28},{2... | collective-permute-start | bytes 1572872 | tf_op jit(solution)/shard_map/ppermute | solution.py:172
  18.2 30.6 %collective-permute-start.8 = (bf16[2,4,256,128]{3,2,1,0:T(8,128)(2,1)S(1)}, bf16[2,4,256,128]{3,2,1,0:T(8,128)(2,1)S(1)}, u32[]{:S(2)}, u32[]{:S(2)}) collective-permute-start(bf16[2,4,256,128]{3,2,1,0:T(8,128)(2,1)S(1)} %collective-permute-done.refs_3_), channel_id=1, source_target_pairs={{0,1},{1,0},{2,3},{3,2},{4,5},{5,4},{6,7},{7,6},{8,9},{9,8},{10,11... | collective-permute-start | bytes 1572872 | tf_op jit(solution)/shard_map/ppermute | solution.py:153
  19.7 19.2 %collective-permute-start.1 = (bf16[2,4,256,128]{3,2,1,0:T(8,128)(2,1)S(1)}, bf16[2,4,256,128]{3,2,1,0:T(8,128)(2,1)S(1)}, u32[]{:S(2)}, u32[]{:S(2)}) collective-permute-start(bf16[2,4,256,128]{3,2,1,0:T(8,128)(2,1)S(1)} %collective-permute-done.refs_3_), channel_id=1, source_target_pairs={{0,4},{4,8},{8,12},{1,5},{5,9},{9,13},{2,6},{6,10},{10,14},{3,7},{... | collective-permute-start | bytes 1572872 | tf_op jit(solution)/shard_map/ppermute | solution.py:163
  23.2 25.6 %collective-permute-start.9 = (bf16[2,4,256,128]{3,2,1,0:T(8,128)(2,1)}, bf16[2,4,256,128]{3,2,1,0:T(8,128)(2,1)S(1)}, u32[]{:S(2)}, u32[]{:S(2)}) collective-permute-start(bf16[2,4,256,128]{3,2,1,0:T(8,128)(2,1)} %collective-permute-done.3.refs_5_), channel_id=1, source_target_pairs={{0,1},{1,0},{2,3},{3,2},{4,5},{5,4},{6,7},{7,6},{8,9},{9,8},{10,11... | collective-permute-start | bytes 1572872 | tf_op jit(solution)/shard_map/ppermute | solution.py:153
  23.5 24.5 %collective-permute-start.4 = (bf16[2,4,256,128]{3,2,1,0:T(8,128)(2,1)}, bf16[2,4,256,128]{3,2,1,0:T(8,128)(2,1)S(1)}, u32[]{:S(2)}, u32[]{:S(2)}) collective-permute-start(bf16[2,4,256,128]{3,2,1,0:T(8,128)(2,1)} %collective-permute-done.3.refs_5_), channel_id=1, source_target_pairs={{4,0},{8,4},{12,8},{5,1},{9,5},{13,9},{6,2},{10,6},{14,10},{7,3},{... | collective-permute-start | bytes 1572872 | tf_op jit(solution)/shard_map/ppermute | solution.py:164
  36.2 29.5 %collective-permute-start.7 = (bf16[2,4,256,128]{3,2,1,0:T(8,128)(2,1)S(1)}, bf16[2,4,256,128]{3,2,1,0:T(8,128)(2,1)S(1)}, u32[]{:S(2)}, u32[]{:S(2)}) collective-permute-start(bf16[2,4,256,128]{3,2,1,0:T(8,128)(2,1)S(1)} %collective-permute-done.6.refs_3_), channel_id=1, source_target_pairs={{0,1},{1,0},{2,3},{3,2},{4,5},{5,4},{6,7},{7,6},{8,9},{9,8},{10,11... | collective-permute-start | bytes 1572872 | tf_op jit(solution)/shard_map/ppermute | solution.py:153
  38.9 47.6 %collective-permute-start.2 = (bf16[2,4,256,128]{3,2,1,0:T(8,128)(2,1)S(1)}, bf16[2,4,256,128]{3,2,1,0:T(8,128)(2,1)S(1)}, u32[]{:S(2)}, u32[]{:S(2)}) collective-permute-start(bf16[2,4,256,128]{3,2,1,0:T(8,128)(2,1)S(1)} %collective-permute-done.1.refs_3_), channel_id=1, source_target_pairs={{0,1},{1,0},{2,3},{3,2},{4,5},{5,4},{6,7},{7,6},{8,9},{9,8},{10,11... | collective-permute-start | bytes 1572872 | tf_op jit(solution)/shard_map/ppermute | solution.py:153
  48.0 38.5 %collective-permute-start.5 = (bf16[2,4,256,128]{3,2,1,0:T(8,128)(2,1)S(1)}, bf16[2,4,256,128]{3,2,1,0:T(8,128)(2,1)S(1)}, u32[]{:S(2)}, u32[]{:S(2)}) collective-permute-start(bf16[2,4,256,128]{3,2,1,0:T(8,128)(2,1)S(1)} %collective-permute-done.4.refs_5_), channel_id=1, source_target_pairs={{0,1},{1,0},{2,3},{3,2},{4,5},{5,4},{6,7},{7,6},{8,9},{9,8},{10,11... | collective-permute-start | bytes 1572872 | tf_op jit(solution)/shard_map/ppermute | solution.py:153
  82.1 2.6 %copy-start = (f32[16,384,256]{2,1,0:T(8,128)}, f32[16,384,256]{2,1,0:T(8,128)S(1)}, u32[]{:S(2)}) copy-start(f32[16,384,256]{2,1,0:T(8,128)S(1)} %get-tuple-element.16.refs_7_) | copy-start | bytes 18874372
  84.8 1.7 %copy-start.1 = (f32[16,384,128]{2,1,0:T(8,128)}, f32[16,384,128]{2,1,0:T(8,128)S(1)}, u32[]{:S(2)}) copy-start(f32[16,384,128]{2,1,0:T(8,128)S(1)} %get-tuple-element.17.refs_8_) | copy-start | bytes 9437188
  86.5 1.9 %copy-start.2 = (f32[16,384,128]{2,1,0:T(8,128)S(1)}, f32[16,384,128]{2,1,0:T(8,128)}, u32[]{:S(2)}) copy-start(f32[16,384,128]{2,1,0:T(8,128)} %copy-done.1) | copy-start | bytes 9437188

commit v2 on v1

--- a/solution.py
+++ b/solution.py
@@ -11,91 +11,129 @@
 NEG = -1e30
 
 
+ONES = 16
+KEEP = 8
+
+
 def attend_kernel(slots, first, last, scale, *refs):
     src_ref, bias_ref, q_ref = refs[:3]
     kv_refs = refs[3 : 3 + 2 * slots]
     rest = refs[3 + 2 * slots :]
+    s_refs = rest[-2:]
+    rest = rest[:-2]
     if first:
         acc_in, top_in = None, None
-        outs = rest
     else:
         acc_in, top_in = rest[:2]
-        outs = rest[2:]
+        rest = rest[2:]
+    if last:
+        out_ref, rest = rest[0], rest[1:]
+    acc_out, top_out = rest
     pairs, rows, width = q_ref.shape
     heads = kv_refs[0].shape[1]
     half = kv_refs[0].shape[2]
     blocks = pairs // heads
-    block_rows = half * 2 // blocks
+    block_rows = 2 * half // blocks
     half_blocks = half // block_rows
     rep = src_ref[0]
-    ones = jnp.ones((half, width), jnp.bfloat16)
-
-    def update(pair, slot, acc_src, top_src, acc_dst, top_dst, fresh):
+    ones = jnp.ones((ONES, 2 * half), jnp.bfloat16)
+
+    def score(pair, slot, s_ref):
+        head = pair // blocks
+        query = q_ref[pair]
+        for part in range(2):
+            s_ref[part * half : (part + 1) * half] = lax.dot_general(
+                kv_refs[2 * slot + part][0, head],
+                query,
+                (((1,), (1,)), ((), ())),
+                preferred_element_type=jnp.float32,
+            )
+
+    def absorb(pair, slot, s_ref, acc_src, top_src):
         head = pair // blocks
         source = src_ref[1 + slot]
-        query = q_ref[pair]
-        scores = []
+        offsets, values = [], []
+        top = None
         for part in range(2):
-            ref = kv_refs[2 * slot + part]
-            raw = lax.dot_general(
-                query, ref[0, head], (((1,), (1,)), ((), ())), preferred_element_type=jnp.float32
-            )
             base = source * blocks + (rep if part == 0 else 1 - rep) * half_blocks
             for piece in range(half_blocks):
-                cut = raw[:, piece * block_rows : (piece + 1) * block_rows]
-                scores.append(cut * scale + bias_ref[pair, base + piece])
-        top = functools.reduce(jnp.maximum, scores)
-        top = jnp.max(top, axis=-1, keepdims=True)
-        if not fresh:
-            before = top_src[pair][:, :1]
+                start = part * half + piece * block_rows
+                offset = bias_ref[pair, base + piece]
+                block = s_ref[start : start + block_rows]
+                peak = jnp.max(block.reshape(block_rows // 8, 8, rows), axis=0) * scale + offset
+                top = peak if top is None else jnp.maximum(top, peak)
+                offsets.append(offset)
+                values.append(
+                    kv_refs[2 * slot + part][1, head, piece * width : (piece + 1) * width, :]
+                )
+        top = jnp.max(top, axis=0, keepdims=True)
+        if acc_src is not None:
+            before = top_src[pair, :1]
             top = jnp.maximum(top, before)
-        weights = [jnp.exp2(piece - top).astype(jnp.bfloat16) for piece in scores]
-        total = None
-        for part in range(2):
-            ref = kv_refs[2 * slot + part]
-            value = jnp.concatenate([ref[1, head], ones], axis=1)
-            weight = jnp.concatenate(
-                weights[part * half_blocks : (part + 1) * half_blocks], axis=1
-            )
-            term = jnp.dot(weight, value, preferred_element_type=jnp.float32)
-            total = term if total is None else total + term
-        if not fresh:
-            total = total + acc_src[pair] * jnp.exp2(before - top)
-        acc_dst[pair] = total
-        top_dst[pair] = jnp.broadcast_to(top, top_dst.shape[1:])
+        weights = []
+        for index, offset in enumerate(offsets):
+            block = s_ref[index * block_rows : (index + 1) * block_rows]
+            weights.append(jnp.exp2(block * scale - (top - offset)).astype(jnp.bfloat16))
+        value = jnp.concatenate([jnp.concatenate(values, axis=1), ones], axis=0)
+        term = jnp.dot(
+            value, jnp.concatenate(weights, axis=0), preferred_element_type=jnp.float32
+        )[: width + KEEP]
+        if acc_src is not None:
+            term = term + acc_src[pair] * jnp.exp2(before - top)
+        acc_out[pair] = term
+        top_out[pair] = jnp.broadcast_to(top, top_out.shape[1:])
+
+    def sweep(slot, acc_src, top_src):
+        score(0, slot, s_refs[0])
+
+        @pl.loop(0, pairs // 2)
+        def _(step):
+            pair = 2 * step
+            score(pair + 1, slot, s_refs[1])
+            absorb(pair, slot, s_refs[0], acc_src, top_src)
+            score(jnp.minimum(pair + 2, pairs - 1), slot, s_refs[0])
+            absorb(pair + 1, slot, s_refs[1], acc_src, top_src)
 
     if first:
-        acc_dst, top_dst = outs[:2]
-    elif last:
-        acc_dst, top_dst = outs[1:3]
+        sweep(0, None, None)
     else:
-        acc_dst, top_dst = outs[:2]
-
-    if first:
+        valid = [src_ref[1 + slot] >= 0 for slot in range(slots)]
+        seen = None
+        for slot in range(slots):
+            if seen is None:
+                pl.when(valid[slot])(functools.partial(sweep, slot, acc_in, top_in))
+                seen = valid[slot]
+            else:
+                fresh = jnp.logical_and(valid[slot], jnp.logical_not(seen))
+                again = jnp.logical_and(valid[slot], seen)
+                pl.when(fresh)(functools.partial(sweep, slot, acc_in, top_in))
+                pl.when(again)(functools.partial(sweep, slot, acc_out, top_out))
+                seen = jnp.logical_or(seen, valid[slot])
+
+        @pl.when(jnp.logical_not(seen))
+        def _():
+            @pl.loop(0, pairs)
+            def _(pair):
+                acc_out[pair] = acc_in[pair]
+                top_out[pair] = top_in[pair]
+
+    if last:
+        row = lax.broadcasted_iota(jnp.int32, (block_rows, block_rows), 0)
+        column = lax.broadcasted_iota(jnp.int32, (block_rows, block_rows), 1)
+        eye = jnp.where(row == column, 1.0, 0.0).astype(jnp.bfloat16)
+
         @pl.loop(0, pairs)
         def _(pair):
-            update(pair, 0, None, None, acc_dst, top_dst, True)
-    else:
-
-        @pl.loop(0, pairs)
-        def _(pair):
-            acc_dst[pair] = acc_in[pair]
-            top_dst[pair] = top_in[pair]
-
-        for slot in range(slots):
-
-            @pl.when(src_ref[1 + slot] >= 0)
-            def _():
-                @pl.loop(0, pairs)
-                def _(pair):
-                    update(pair, slot, acc_dst, top_dst, acc_dst, top_dst, False)
-    if last:
-        out_ref = outs[0]
-
-        @pl.loop(0, pairs)
-        def _(pair):
-            total = acc_dst[pair]
-            out_ref[pair] = (total[:, :width] / total[:, width:]).astype(out_ref.dtype)
+            total = acc_out[pair]
+            value = (total[:width] / total[width : width + 1]).astype(jnp.bfloat16)
+            for piece in range(rows // block_rows):
+                cut = slice(piece * block_rows, (piece + 1) * block_rows)
+                out_ref[pair, cut] = lax.dot_general(
+                    eye,
+                    value[:, cut],
+                    (((1,), (1,)), ((), ())),
+                    preferred_element_type=jnp.float32,
+                ).astype(out_ref.dtype)
 
 
 def attend_call(sources, bias, query, kv, state, last, scale):
@@ -107,26 +145,23 @@
     operands = [sources, bias, query, *kv]
     specs = [smem, smem] + [vmem] * (1 + len(kv))
     shapes = [
-        jax.ShapeDtypeStruct((pairs, rows, 2 * width), jnp.float32),
-        jax.ShapeDtypeStruct((pairs, rows, width), jnp.float32),
+        jax.ShapeDtypeStruct((pairs, width + KEEP, rows), jnp.float32),
+        jax.ShapeDtypeStruct((pairs, KEEP, rows), jnp.float32),
     ]
-    aliases = {}
     if not first:
-        aliases = {len(operands): 0, len(operands) + 1: 1}
         operands += list(state)
         specs += [vmem, vmem]
     if last:
         shapes = [jax.ShapeDtypeStruct((pairs, rows, width), jnp.bfloat16)] + shapes
-        aliases = {key: value + 1 for key, value in aliases.items()}
-    keys = slots * 2 * kv[0].shape[2]
-    work = pairs * rows * keys
+    keys = 2 * kv[0].shape[2]
+    work = pairs * rows * keys * slots
     return pl.pallas_call(
         functools.partial(attend_kernel, slots, first, last, scale),
         out_shape=shapes,
         in_specs=specs,
         out_specs=[vmem] * len(shapes),
-        input_output_aliases=aliases,
-        compiler_params=pltpu.CompilerParams(vmem_limit_bytes=40 << 20),
+        scratch_shapes=[pltpu.VMEM((keys, rows), jnp.float32)] * 2,
+        compiler_params=pltpu.CompilerParams(vmem_limit_bytes=24 << 20),
         cost_estimate=pl.CostEstimate(
             flops=6 * work * width, bytes_accessed=4 * pairs * rows * width, transcendentals=work
         ),
@@ -147,7 +182,10 @@
     def half_of(which):
         key_half = lax.dynamic_slice_in_dim(key_rows, which * half, half, 0)
         value_half = lax.dynamic_slice_in_dim(value_rows, which * half, half, 0)
-        return jnp.transpose(jnp.stack([key_half, value_half]), (0, 2, 1, 3))
+        key_half = jnp.transpose(key_half, (1, 0, 2))
+        value_half = value_half.reshape(half // block_rows, block_rows, heads, width)
+        value_half = jnp.transpose(value_half, (2, 0, 3, 1)).reshape(key_half.shape)
+        return jnp.stack([key_half, value_half])
 
     def swap(array):
         return lax.ppermute(array, "rep", [(0, 1), (1, 0)])

time: 113 us -> 75.5 us (0.67)
  Pallas kernels: 66.2 us -> 29.5 us
  local copies, waits for them, and re-layouts: 12.9 us -> 7.04 us
  waiting for transfers between devices: 9.95 us -> 14 us
  starting transfers between devices: 21.3 us -> 22.6 us
    pallas_call x4, Pallas kernels: 66.2 us -> 29.5 us  [attend_call(): pl.pallas_call(functools.partial(attend_kernel, slots, first, last, scale...]
    unnamed x14 -> x12, local copies, waits for them, and re-layouts: 6.27 us -> 0.87 us
    ppermute x1, waiting for transfers between devices: 0.01 us -> 2.92 us  [local(): far = lax.ppermute(mine, 'ctx', [(0, ctx_count - 1), (ctx_count - 1, 0)])]
    ppermute x5, starting transfers between devices: 4.51 us -> 6.02 us  [swap(): return lax.ppermute(array, 'rep', [(0, 1), (1, 0)])]
    ppermute x2, waiting for transfers between devices: 2.36 us -> 3.54 us  [local(): from_left = lax.ppermute(from_left, 'ctx', right)]
  transfers between devices with their start and end apart: 10 -> 10, of which waited for: 2 -> 3; matrix products, arithmetic and copies ran while one was open for 4% -> 6% of each run, Pallas kernels for 40% -> 24%
where the time goes in v2:
time: 75.5 us; the launch traced here: 75.2 us
  Pallas kernels  29.5 us (39%)
  starting transfers between devices  22.6 us (30%)
  waiting for transfers between devices  14 us (19%)
  local copies, waits for them, and re-layouts  7.04 us (9%)
  other arithmetic  1.73 us (2%)
    pallas_call x4, Pallas kernels, attend_call(): pl.pallas_call(functools.partial(attend_kernel, slots, first, last, scale...  29.5 us
    ppermute x2, waiting for transfers between devices, local(): from_right = lax.ppermute(from_right, 'ctx', left)  7.58 us
    ppermute x2, starting transfers between devices, local(): from_left = lax.ppermute(from_left, 'ctx', right)  7.28 us
    ppermute x1, starting transfers between devices, local(): far = lax.ppermute(mine, 'ctx', [(0, ctx_count - 1), (ctx_count - 1, 0)])  6.77 us
    ppermute x5, starting transfers between devices, swap(): return lax.ppermute(array, 'rep', [(0, 1), (1, 0)])  6.02 us
    ppermute x2, waiting for transfers between devices, local(): from_left = lax.ppermute(from_left, 'ctx', right)  3.54 us
    ppermute x1, waiting for transfers between devices, local(): far = lax.ppermute(mine, 'ctx', [(0, ctx_count - 1), (ctx_count - 1, 0)])  2.92 us
    ppermute x2, starting transfers between devices, local(): from_right = lax.ppermute(from_right, 'ctx', left)  2.57 us
  transfers between devices with their start and end apart: 10, of which 3 were waited for; matrix products, arithmetic and copies ran while one was open for 6% of the time, Pallas kernels for 24%

profile of v2, /device:TPU:1, one launch (start us, length us, event | category | flops | bytes accessed | tf_op | source)
XLA Modules:
  0.0 75.2 jit_solution(2521652110615605662)
XLA Ops:
  0.0 1.6 %constant_dynamic-slice_fusion = (bf16[256,4,128]{2,1,0:T(4,128)(2,1)S(1)}, bf16[256,4,128]{2,1,0:T(4,128)(2,1)S(1)}, bf16[256,4,128]{2,1,0:T(4,128)(2,1)S(1)}, bf16[256,4,128]{2,1,0:T(4,128)(2,1)S(1)}) fusion(bf16[512,4,128]{2,1,0:T(4,128)(2,1)} %param.9, s32[]{:T(128)S(6)} %select_n.51, s32[]{:T(128)S(6)} %select_n.47, bf16[512,4,128]{2,1,0:T(4,128)(2,1)} %param.8), kind=kLoop, calls=%fused_computation.27 | loop fusion | bytes 2097160 | tf_op jit(solution)/shard_map/dynamic_slice | solution.py:184
  1.7 0.2 copy.25
  1.9 4.1 %collective-permute-start = (bf16[2,4,256,128]{3,2,1,0:T(8,128)(2,1)S(1)}, bf16[2,4,256,128]{3,2,1,0:T(8,128)(2,1)S(1)}, u32[]{:S(2)}, u32[]{:S(2)}) collective-permute-start(bf16[2,4,256,128]{3,2,1,0:T(8,128)(2,1)S(1)} %pad_maximum_fusion.refs_3_), channel_id=1, source_target_pairs={{0,4},{4,8},{8,12},{1,5},{5,9},{9,13},{2,6},{6,10},{10,14},{3,7},{... | collective-permute-start | bytes 1572872 | tf_op jit(solution)/shard_map/ppermute | solution.py:201
  6.0 1.3 %collective-permute-start.3 = (bf16[2,4,256,128]{3,2,1,0:T(8,128)(2,1)S(1)}, bf16[2,4,256,128]{3,2,1,0:T(8,128)(2,1)}, u32[]{:S(2)}, u32[]{:S(2)}) collective-permute-start(bf16[2,4,256,128]{3,2,1,0:T(8,128)(2,1)S(1)} %pad_maximum_fusion.refs_3_), channel_id=1, source_target_pairs={{4,0},{8,4},{12,8},{5,1},{9,5},{13,9},{6,2},{10,6},{14,10},{7,3},{... | collective-permute-start | bytes 1572872 | tf_op jit(solution)/shard_map/ppermute | solution.py:202
  7.3 6.8 %collective-permute-start.6 = (bf16[2,4,256,128]{3,2,1,0:T(8,128)(2,1)S(1)}, bf16[2,4,256,128]{3,2,1,0:T(8,128)(2,1)S(1)}, u32[]{:S(2)}, u32[]{:S(2)}) collective-permute-start(bf16[2,4,256,128]{3,2,1,0:T(8,128)(2,1)S(1)} %pad_maximum_fusion.refs_3_), channel_id=1, source_target_pairs={{0,12},{12,0},{1,13},{13,1},{2,14},{14,2},{3,15},{15,3},{16,28},{2... | collective-permute-start | bytes 1572872 | tf_op jit(solution)/shard_map/ppermute | solution.py:210
  14.1 0.2 copy.28
  14.3 0.7 copy.36
  15.2 1.8 %copy.22 = bf16[4,128,4,3,128]{4,1,3,0,2:T(8,128)(2,1)S(1)} copy(bf16[4,128,4,3,128]{4,2,3,1,0:T(4,128)(2,1)} %bitcast.43) | data formatting | bytes 3145728 | tf_op jit(solution)/shard_map/reshape | solution.py:232
  17.5 1.0 %pad_maximum_fusion.1.refs_4_ = bf16[2,4,256,128]{3,2,1,0:T(8,128)(2,1)S(1)} fusion(bf16[1,4,256,128]{3,2,1,0:T(8,128)(2,1)S(1)} %bitcast.46, bf16[1,4,256,128]{3,2,1,0:T(8,128)(2,1)} %bitcast.47), kind=kLoop, calls=%fused_computation.1 | loop fusion | flops 262144 | bytes 1048576 | tf_op jit(solution)/shard_map/stack | solution.py:188
  18.6 1.5 %collective-permute-start.8 = (bf16[2,4,256,128]{3,2,1,0:T(8,128)(2,1)S(1)}, bf16[2,4,256,128]{3,2,1,0:T(8,128)(2,1)S(1)}, u32[]{:S(2)}, u32[]{:S(2)}) collective-permute-start(bf16[2,4,256,128]{3,2,1,0:T(8,128)(2,1)S(1)} %collective-permute-done.refs_3_), channel_id=1, source_target_pairs={{0,1},{1,0},{2,3},{3,2},{4,5},{5,4},{6,7},{7,6},{8,9},{9,8},{10,11... | collective-permute-start | bytes 1572872 | tf_op jit(solution)/shard_map/ppermute | solution.py:191
  20.1 3.2 %collective-permute-start.1 = (bf16[2,4,256,128]{3,2,1,0:T(8,128)(2,1)S(1)}, bf16[2,4,256,128]{3,2,1,0:T(8,128)(2,1)S(1)}, u32[]{:S(2)}, u32[]{:S(2)}) collective-permute-start(bf16[2,4,256,128]{3,2,1,0:T(8,128)(2,1)S(1)} %collective-permute-done.refs_3_), channel_id=1, source_target_pairs={{0,4},{4,8},{8,12},{1,5},{5,9},{9,13},{2,6},{6,10},{10,14},{3,7},{... | collective-permute-start | bytes 1572872 | tf_op jit(solution)/shard_map/ppermute | solution.py:201
  23.4 0.3 collective-permute-start.9
  23.7 1.3 %collective-permute-start.4 = (bf16[2,4,256,128]{3,2,1,0:T(8,128)(2,1)}, bf16[2,4,256,128]{3,2,1,0:T(8,128)(2,1)S(1)}, u32[]{:S(2)}, u32[]{:S(2)}) collective-permute-start(bf16[2,4,256,128]{3,2,1,0:T(8,128)(2,1)} %collective-permute-done.3.refs_5_), channel_id=1, source_target_pairs={{4,0},{8,4},{12,8},{5,1},{9,5},{13,9},{6,2},{10,6},{14,10},{7,3},{... | collective-permute-start | bytes 1572872 | tf_op jit(solution)/shard_map/ppermute | solution.py:202
  25.0 5.7 %shard_map.73 = (f32[16,136,384]{2,1,0:T(8,128)S(1)}, f32[16,8,384]{2,1,0:T(8,128)S(1)}) custom-call(s32[2]{0:T(128)S(1)} %pad_add_fusion.3.refs_0_, f32[16,16]{1,0:T(8,128)S(1)} %bitcast.39, bf16[16,384,128]{2,1,0:T(8,128)(2,1)S(1)} %bitcast.34, bf16[2,4,256,128]{3,2,1,0:T(8,128)(2,1)S(1)} %pad_maximum_fusion.refs_3_, ...), custom_call_target="tpu_custom_call" | custom-call | flops 2415919104 | bytes 3145728 | tf_op jit(solution)/shard_map/pallas_call | solution.py:158
  30.7 2.9 %collective-permute-done.6.refs_3_ = bf16[2,4,256,128]{3,2,1,0:T(8,128)(2,1)S(1)} collective-permute-done((bf16[2,4,256,128]{3,2,1,0:T(8,128)(2,1)S(1)}, bf16[2,4,256,128]{3,2,1,0:T(8,128)(2,1)S(1)}, u32[]{:S(2)}, u32[]{:S(2)}) %collective-permute-start.6) | collective-permute-done | bytes 524320 | tf_op jit(solution)/shard_map/ppermute | solution.py:210
  33.7 1.8 %collective-permute-start.7 = (bf16[2,4,256,128]{3,2,1,0:T(8,128)(2,1)S(1)}, bf16[2,4,256,128]{3,2,1,0:T(8,128)(2,1)S(1)}, u32[]{:S(2)}, u32[]{:S(2)}) collective-permute-start(bf16[2,4,256,128]{3,2,1,0:T(8,128)(2,1)S(1)} %collective-permute-done.6.refs_3_), channel_id=1, source_target_pairs={{0,1},{1,0},{2,3},{3,2},{4,5},{5,4},{6,7},{7,6},{8,9},{9,8},{10,11... | collective-permute-start | bytes 1572872 | tf_op jit(solution)/shard_map/ppermute | solution.py:191
  35.5 3.5 %collective-permute-done.1.refs_3_ = bf16[2,4,256,128]{3,2,1,0:T(8,128)(2,1)S(1)} collective-permute-done((bf16[2,4,256,128]{3,2,1,0:T(8,128)(2,1)S(1)}, bf16[2,4,256,128]{3,2,1,0:T(8,128)(2,1)S(1)}, u32[]{:S(2)}, u32[]{:S(2)}) %collective-permute-start.1) | collective-permute-done | bytes 524320 | tf_op jit(solution)/shard_map/ppermute | solution.py:201
  39.1 1.5 %collective-permute-start.2 = (bf16[2,4,256,128]{3,2,1,0:T(8,128)(2,1)S(1)}, bf16[2,4,256,128]{3,2,1,0:T(8,128)(2,1)S(1)}, u32[]{:S(2)}, u32[]{:S(2)}) collective-permute-start(bf16[2,4,256,128]{3,2,1,0:T(8,128)(2,1)S(1)} %collective-permute-done.1.refs_3_), channel_id=1, source_target_pairs={{0,1},{1,0},{2,3},{3,2},{4,5},{5,4},{6,7},{7,6},{8,9},{9,8},{10,11... | collective-permute-start | bytes 1572872 | tf_op jit(solution)/shard_map/ppermute | solution.py:191
  40.6 7.6 %collective-permute-done.4.refs_5_ = bf16[2,4,256,128]{3,2,1,0:T(8,128)(2,1)S(1)} collective-permute-done((bf16[2,4,256,128]{3,2,1,0:T(8,128)(2,1)}, bf16[2,4,256,128]{3,2,1,0:T(8,128)(2,1)S(1)}, u32[]{:S(2)}, u32[]{:S(2)}) %collective-permute-start.4) | collective-permute-done | bytes 524320 | tf_op jit(solution)/shard_map/ppermute | solution.py:202
  48.2 0.8 %collective-permute-start.5 = (bf16[2,4,256,128]{3,2,1,0:T(8,128)(2,1)S(1)}, bf16[2,4,256,128]{3,2,1,0:T(8,128)(2,1)S(1)}, u32[]{:S(2)}, u32[]{:S(2)}) collective-permute-start(bf16[2,4,256,128]{3,2,1,0:T(8,128)(2,1)S(1)} %collective-permute-done.4.refs_5_), channel_id=1, source_target_pairs={{0,1},{1,0},{2,3},{3,2},{4,5},{5,4},{6,7},{7,6},{8,9},{9,8},{10,11... | collective-permute-start | bytes 1572872 | tf_op jit(solution)/shard_map/ppermute | solution.py:191
  49.0 6.6 %shard_map.74 = (f32[16,136,384]{2,1,0:T(8,128)S(1)}, f32[16,8,384]{2,1,0:T(8,128)S(1)}) custom-call(s32[3]{0:T(128)S(1)} %pad_add_fusion.2.refs_0_, f32[16,16]{1,0:T(8,128)S(1)} %bitcast.40, bf16[16,384,128]{2,1,0:T(8,128)(2,1)S(1)} %bitcast.35, bf16[2,4,256,128]{3,2,1,0:T(8,128)(2,1)S(1)} %collective-permute-done.refs_3_, ...), custom_call_target="tpu_custom_call" | custom-call | flops 4831838208 | bytes 3145728 | tf_op jit(solution)/shard_map/pallas_call | solution.py:158
  55.6 6.1 %shard_map.75 = (f32[16,136,384]{2,1,0:T(8,128)S(1)}, f32[16,8,384]{2,1,0:T(8,128)S(1)}) custom-call(s32[2]{0:T(128)S(1)} %pad_add_fusion.1.refs_0_, f32[16,16]{1,0:T(8,128)S(1)} %bitcast.41, bf16[16,384,128]{2,1,0:T(8,128)(2,1)S(1)} %bitcast.36, bf16[2,4,256,128]{3,2,1,0:T(8,128)(2,1)S(1)} %collective-permute-done.6.refs_3_, ...), custom_call_target="tpu_custom_call" | custom-call | flops 2415919104 | bytes 3145728 | tf_op jit(solution)/shard_map/pallas_call | solution.py:158
  61.7 11.1 %shard_map.76 = (bf16[16,384,128]{2,1,0:T(8,128)(2,1)S(1)}, f32[16,136,384]{2,1,0:T(8,128)}, f32[16,8,384]{2,1,0:T(8,128)}) custom-call(s32[3]{0:T(128)S(1)} %pad_add_fusion.refs_0_, f32[16,16]{1,0:T(8,128)S(1)} %bitcast.42, bf16[16,384,128]{2,1,0:T(8,128)(2,1)S(1)} %bitcast.37, bf16[2,4,256,128]{3,2,1,0:T(8,128)(2,1)S(1)} %collective-permute-done.1.refs_3_, ...), custom_call_target="tpu_custom_call" | custom-call | flops 4831838208 | bytes 3145728 | tf_op jit(solution)/shard_map/pallas_call | solution.py:158
  72.8 2.4 %copy.29 = bf16[4,128,4,3,128]{4,2,3,1,0:T(4,128)(2,1)} copy(bf16[4,128,4,3,128]{4,1,3,0,2:T(8,128)(2,1)S(1)} %bitcast.38) | data formatting | bytes 3145728 | tf_op jit(solution)/shard_map/transpose | solution.py:261
  (32 shorter events, 1.0 us)
Async XLA Ops:
  0.0 15.1 %copy-start.2 = (s32[16]{0:T(128)S(1)}, s32[16]{0:T(128)}, u32[]{:S(2)}) copy-start(s32[16]{0:T(128)} %param.10) | copy-start | bytes 196
  0.0 15.2 %copy-start.3 = (s32[16]{0:T(128)S(1)}, s32[16]{0:T(128)}, u32[]{:S(2)}) copy-start(s32[16]{0:T(128)} %param.12) | copy-start | bytes 196
  0.0 15.2 %copy-start = (s32[4,4]{1,0:T(4,128)S(1)}, s32[4,4]{1,0:T(4,128)}, u32[]{:S(2)}) copy-start(s32[4,4]{1,0:T(4,128)} %param.13) | copy-start | bytes 196
  1.6 15.5 %copy-start.1 = (s32[16,4]{0,1:T(4,128)S(1)}, s32[16,4]{0,1:T(4,128)}, u32[]{:S(2)}) copy-start(s32[16,4]{0,1:T(4,128)} %param.11) | copy-start | bytes 772
  1.9 16.6 %collective-permute-start = (bf16[2,4,256,128]{3,2,1,0:T(8,128)(2,1)S(1)}, bf16[2,4,256,128]{3,2,1,0:T(8,128)(2,1)S(1)}, u32[]{:S(2)}, u32[]{:S(2)}) collective-permute-start(bf16[2,4,256,128]{3,2,1,0:T(8,128)(2,1)S(1)} %pad_maximum_fusion.refs_3_), channel_id=1, source_target_pairs={{0,4},{4,8},{8,12},{1,5},{5,9},{9,13},{2,6},{6,10},{10,14},{3,7},{... | collective-permute-start | bytes 1572872 | tf_op jit(solution)/shard_map/ppermute | solution.py:201
  6.0 17.4 %collective-permute-start.3 = (bf16[2,4,256,128]{3,2,1,0:T(8,128)(2,1)S(1)}, bf16[2,4,256,128]{3,2,1,0:T(8,128)(2,1)}, u32[]{:S(2)}, u32[]{:S(2)}) collective-permute-start(bf16[2,4,256,128]{3,2,1,0:T(8,128)(2,1)S(1)} %pad_maximum_fusion.refs_3_), channel_id=1, source_target_pairs={{4,0},{8,4},{12,8},{5,1},{9,5},{13,9},{6,2},{10,6},{14,10},{7,3},{... | collective-permute-start | bytes 1572872 | tf_op jit(solution)/shard_map/ppermute | solution.py:202
  7.3 26.4 %collective-permute-start.6 = (bf16[2,4,256,128]{3,2,1,0:T(8,128)(2,1)S(1)}, bf16[2,4,256,128]{3,2,1,0:T(8,128)(2,1)S(1)}, u32[]{:S(2)}, u32[]{:S(2)}) collective-permute-start(bf16[2,4,256,128]{3,2,1,0:T(8,128)(2,1)S(1)} %pad_maximum_fusion.refs_3_), channel_id=1, source_target_pairs={{0,12},{12,0},{1,13},{13,1},{2,14},{14,2},{3,15},{15,3},{16,28},{2... | collective-permute-start | bytes 1572872 | tf_op jit(solution)/shard_map/ppermute | solution.py:210
  18.6 30.4 %collective-permute-start.8 = (bf16[2,4,256,128]{3,2,1,0:T(8,128)(2,1)S(1)}, bf16[2,4,256,128]{3,2,1,0:T(8,128)(2,1)S(1)}, u32[]{:S(2)}, u32[]{:S(2)}) collective-permute-start(bf16[2,4,256,128]{3,2,1,0:T(8,128)(2,1)S(1)} %collective-permute-done.refs_3_), channel_id=1, source_target_pairs={{0,1},{1,0},{2,3},{3,2},{4,5},{5,4},{6,7},{7,6},{8,9},{9,8},{10,11... | collective-permute-start | bytes 1572872 | tf_op jit(solution)/shard_map/ppermute | solution.py:191
  20.1 19.0 %collective-permute-start.1 = (bf16[2,4,256,128]{3,2,1,0:T(8,128)(2,1)S(1)}, bf16[2,4,256,128]{3,2,1,0:T(8,128)(2,1)S(1)}, u32[]{:S(2)}, u32[]{:S(2)}) collective-permute-start(bf16[2,4,256,128]{3,2,1,0:T(8,128)(2,1)S(1)} %collective-permute-done.refs_3_), channel_id=1, source_target_pairs={{0,4},{4,8},{8,12},{1,5},{5,9},{9,13},{2,6},{6,10},{10,14},{3,7},{... | collective-permute-start | bytes 1572872 | tf_op jit(solution)/shard_map/ppermute | solution.py:201
  23.4 25.6 %collective-permute-start.9 = (bf16[2,4,256,128]{3,2,1,0:T(8,128)(2,1)}, bf16[2,4,256,128]{3,2,1,0:T(8,128)(2,1)S(1)}, u32[]{:S(2)}, u32[]{:S(2)}) collective-permute-start(bf16[2,4,256,128]{3,2,1,0:T(8,128)(2,1)} %collective-permute-done.3.refs_5_), channel_id=1, source_target_pairs={{0,1},{1,0},{2,3},{3,2},{4,5},{5,4},{6,7},{7,6},{8,9},{9,8},{10,11... | collective-permute-start | bytes 1572872 | tf_op jit(solution)/shard_map/ppermute | solution.py:191
  23.7 24.5 %collective-permute-start.4 = (bf16[2,4,256,128]{3,2,1,0:T(8,128)(2,1)}, bf16[2,4,256,128]{3,2,1,0:T(8,128)(2,1)S(1)}, u32[]{:S(2)}, u32[]{:S(2)}) collective-permute-start(bf16[2,4,256,128]{3,2,1,0:T(8,128)(2,1)} %collective-permute-done.3.refs_5_), channel_id=1, source_target_pairs={{4,0},{8,4},{12,8},{5,1},{9,5},{13,9},{6,2},{10,6},{14,10},{7,3},{... | collective-permute-start | bytes 1572872 | tf_op jit(solution)/shard_map/ppermute | solution.py:202
  33.7 21.9 %collective-permute-start.7 = (bf16[2,4,256,128]{3,2,1,0:T(8,128)(2,1)S(1)}, bf16[2,4,256,128]{3,2,1,0:T(8,128)(2,1)S(1)}, u32[]{:S(2)}, u32[]{:S(2)}) collective-permute-start(bf16[2,4,256,128]{3,2,1,0:T(8,128)(2,1)S(1)} %collective-permute-done.6.refs_3_), channel_id=1, source_target_pairs={{0,1},{1,0},{2,3},{3,2},{4,5},{5,4},{6,7},{7,6},{8,9},{9,8},{10,11... | collective-permute-start | bytes 1572872 | tf_op jit(solution)/shard_map/ppermute | solution.py:191
  39.1 22.6 %collective-permute-start.2 = (bf16[2,4,256,128]{3,2,1,0:T(8,128)(2,1)S(1)}, bf16[2,4,256,128]{3,2,1,0:T(8,128)(2,1)S(1)}, u32[]{:S(2)}, u32[]{:S(2)}) collective-permute-start(bf16[2,4,256,128]{3,2,1,0:T(8,128)(2,1)S(1)} %collective-permute-done.1.refs_3_), channel_id=1, source_target_pairs={{0,1},{1,0},{2,3},{3,2},{4,5},{5,4},{6,7},{7,6},{8,9},{9,8},{10,11... | collective-permute-start | bytes 1572872 | tf_op jit(solution)/shard_map/ppermute | solution.py:191
  48.2 13.5 %collective-permute-start.5 = (bf16[2,4,256,128]{3,2,1,0:T(8,128)(2,1)S(1)}, bf16[2,4,256,128]{3,2,1,0:T(8,128)(2,1)S(1)}, u32[]{:S(2)}, u32[]{:S(2)}) collective-permute-start(bf16[2,4,256,128]{3,2,1,0:T(8,128)(2,1)S(1)} %collective-permute-done.4.refs_5_), channel_id=1, source_target_pairs={{0,1},{1,0},{2,3},{3,2},{4,5},{5,4},{6,7},{7,6},{8,9},{9,8},{10,11... | collective-permute-start | bytes 1572872 | tf_op jit(solution)/shard_map/ppermute | solution.py:191

commit v3 on v2

v3 whole, which is shorter than its diff:
```python
import functools
import math

import jax
import jax.numpy as jnp
from jax import lax
from jax.experimental import pallas as pl
from jax.experimental.pallas import tpu as pltpu
from jax.sharding import PartitionSpec as P


NEG = -1e30


ONES = 16
KEEP = 8
PACK = 2


def attend_kernel(units, heads, first, last, scale, *refs):
    src_ref, bias_ref, q_ref = refs[:3]
    slots = len(units)
    kv_refs, rest = [], refs[3:]
    for _, parts in units:
        kv_refs.append(rest[: len(parts)])
        rest = rest[len(parts) :]
    s_refs = rest[-2:]
    rest = rest[:-2]
    acc_in, top_in, out_ref, acc_out, top_out = None, None, None, None, None
    if not first:
        acc_in, top_in = rest[:2]
        rest = rest[2:]
    if last:
        out_ref, rest = rest[0], rest[1:]
    acc_out, top_out = rest
    works, rows, width = q_ref.shape
    half = kv_refs[0][0].shape[2]
    blocks = works * PACK // heads
    block_rows = 2 * half // blocks
    half_blocks = half // block_rows
    rep = src_ref[0]

    def score(work, slot, s_ref):
        head = work * PACK // blocks
        keys = [kv_ref[0, head] for kv_ref in kv_refs[slot]]
        s_ref[: half * len(keys)] = lax.dot_general(
            jnp.concatenate(keys, axis=0),
            q_ref[work],
            (((1,), (1,)), ((), ())),
            preferred_element_type=jnp.float32,
        )

    def finish(work, total):
        value = (total[:width] * (1.0 / total[width : width + 1])).astype(jnp.bfloat16)
        row = lax.broadcasted_iota(jnp.int32, (width, width), 0)
        column = lax.broadcasted_iota(jnp.int32, (width, width), 1)
        eye = jnp.where(row == column, 1.0, 0.0).astype(jnp.bfloat16)
        for piece in range(rows // width):
            cut = slice(piece * width, (piece + 1) * width)
            out_ref[work, cut] = lax.dot_general(
                eye, value[:, cut], (((1,), (1,)), ((), ())), preferred_element_type=jnp.float32
            ).astype(out_ref.dtype)

    def absorb(work, slot, s_ref, acc_src, top_src, final):
        head = work * PACK // blocks
        source = src_ref[units[slot][0]]
        offsets, values = [], []
        top = None
        for part, kv_ref in enumerate(kv_refs[slot]):
            base = source * blocks + (rep if units[slot][1][part] == 0 else 1 - rep) * half_blocks
            for piece in range(half_blocks):
                start = part * half + piece * block_rows
                offset = jnp.concatenate(
                    [
                        jnp.full((1, rows // PACK), bias_ref[work * PACK + index, base + piece])
                        for index in range(PACK)
                    ],
                    axis=1,
                )
                block = s_ref[start : start + block_rows]
                peak = jnp.max(block.reshape(block_rows // 8, 8, rows), axis=0) * scale + offset
                top = peak if top is None else jnp.maximum(top, peak)
                offsets.append(offset)
                values.append(kv_ref[1, head, piece * width : (piece + 1) * width, :])
        top = jnp.max(top, axis=0, keepdims=True)
        if acc_src is not None:
            before = top_src[work, :1]
            top = jnp.maximum(top, before)
        weights = []
        for index, offset in enumerate(offsets):
            block = s_ref[index * block_rows : (index + 1) * block_rows]
            weights.append(jnp.exp2(block * scale - (top - offset)).astype(jnp.bfloat16))
        value = jnp.concatenate(values, axis=1)
        ones = jnp.ones((ONES, value.shape[1]), value.dtype)
        value = jnp.concatenate([value, ones], axis=0)
        term = jnp.dot(
            value, jnp.concatenate(weights, axis=0), preferred_element_type=jnp.float32
        )[: width + KEEP]
        if acc_src is not None:
            term = term + acc_src[work] * jnp.exp2(before - top)
        if final:
            finish(work, term)
        else:
            acc_out[work] = term
            top_out[work] = jnp.broadcast_to(top, top_out.shape[1:])

    def sweep(slot, acc_src, top_src, final):
        score(0, slot, s_refs[0])

        @pl.loop(0, works // 2)
        def _(step):
            work = 2 * step
            score(work + 1, slot, s_refs[1])
            absorb(work, slot, s_refs[0], acc_src, top_src, final)
            score(jnp.minimum(work + 2, works - 1), slot, s_refs[0])
            absorb(work + 1, slot, s_refs[1], acc_src, top_src, final)

    if first:
        sweep(0, None, None, False)
        return
    valid = [src_ref[units[slot][0]] >= 0 for slot in range(slots)]
    seen = None
    for slot in range(slots):
        later = None
        for other in valid[slot + 1 :]:
            later = other if later is None else jnp.logical_or(later, other)
        starts = [(valid[slot], acc_in, top_in)]
        if seen is not None:
            starts = [
                (jnp.logical_and(valid[slot], jnp.logical_not(seen)), acc_in, top_in),
                (jnp.logical_and(valid[slot], seen), acc_out, top_out),
            ]
        for condition, acc_src, top_src in starts:
            if not last or later is None:
                pl.when(condition)(functools.partial(sweep, slot, acc_src, top_src, last))
            else:
                pl.when(jnp.logical_and(condition, later))(
                    functools.partial(sweep, slot, acc_src, top_src, False)
                )
                pl.when(jnp.logical_and(condition, jnp.logical_not(later)))(
                    functools.partial(sweep, slot, acc_src, top_src, True)
                )
        seen = valid[slot] if seen is None else jnp.logical_or(seen, valid[slot])

    @pl.when(jnp.logical_not(seen))
    def _():
        @pl.loop(0, works)
        def _(work):
            if last:
                finish(work, acc_in[work])
            else:
                acc_out[work] = acc_in[work]
                top_out[work] = top_in[work]


def attend_call(sources, bias, query, units, kv, state, last, scale):
    works, rows, width = query.shape
    first = state is None
    vmem = pl.BlockSpec(memory_space=pltpu.VMEM)
    smem = pl.BlockSpec(memory_space=pltpu.SMEM)
    operands = [sources, bias, query, *kv]
    specs = [smem, smem] + [vmem] * (1 + len(kv))
    shapes = [
        jax.ShapeDtypeStruct((works, width + KEEP, rows), jnp.float32),
        jax.ShapeDtypeStruct((works, KEEP, rows), jnp.float32),
    ]
    if not first:
        operands += list(state)
        specs += [vmem, vmem]
    if last:
        shapes = [jax.ShapeDtypeStruct((works, rows, width), jnp.bfloat16)] + shapes
    keys = max(len(parts) for _, parts in units) * kv[0].shape[2]
    work = works * rows * kv[0].shape[2] * len(kv)
    return pl.pallas_call(
        functools.partial(attend_kernel, units, kv[0].shape[1], first, last, scale),
        out_shape=shapes,
        in_specs=specs,
        out_specs=[vmem] * len(shapes),
        scratch_shapes=[pltpu.VMEM((keys, rows), jnp.float32)] * 2,
        compiler_params=pltpu.CompilerParams(vmem_limit_bytes=24 << 20),
        cost_estimate=pl.CostEstimate(
            flops=6 * work * width, bytes_accessed=4 * works * rows * width, transcendentals=work
        ),
    )(*operands)


def run(query_rows, key_rows, value_rows, dest_block, tile_list, tile_count, stripe_start):
    ctx_count = lax.axis_size("ctx")
    ctx_index = lax.axis_index("ctx")
    rep_index = lax.axis_index("rep")
    tok_rows, heads, group, width = query_rows.shape
    block_total = dest_block.shape[0]
    blocks = block_total // ctx_count
    block_rows = tok_rows // blocks
    half = tok_rows // 2
    scale = width ** (-0.5) * math.log2(math.e)

    def half_of(which):
        key_half = lax.dynamic_slice_in_dim(key_rows, which * half, half, 0)
        value_half = lax.dynamic_slice_in_dim(value_rows, which * half, half, 0)
        key_half = jnp.transpose(key_half, (1, 0, 2))
        value_half = value_half.reshape(half // block_rows, block_rows, heads, width)
        value_half = jnp.transpose(value_half, (2, 0, 3, 1)).reshape(key_half.shape)
        return jnp.stack([key_half, value_half])

    mine = half_of(rep_index)
    right = [(i, i + 1) for i in range(ctx_count - 1)]
    left = [(i + 1, i) for i in range(ctx_count - 1)]
    ends = [(0, ctx_count - 1), (ctx_count - 1, 0)]
    from_left = lax.ppermute(mine, "ctx", right)
    from_right = lax.ppermute(mine, "ctx", left)

    owner = dest_block // blocks
    stripes = jnp.sum(
        (stripe_start[:, :, None] // tok_rows == owner[None, None, :]).astype(jnp.int32), axis=1
    )
    placed = lax.dynamic_slice_in_dim(dest_block, ctx_index * blocks, blocks, 0)
    row_pick = (placed[:, None] == jnp.arange(block_total)[None, :]).astype(jnp.int32)
    used = jnp.arange(tile_list.shape[1])[None, :] < tile_count[:, None]
    listed = jnp.sum(
        (used[:, :, None] & (tile_list[:, :, None] == dest_block[None, None, :])).astype(jnp.int32),
        axis=1,
    )
    near = jnp.sum(row_pick[:, :, None] * listed[None], axis=1)
    count = stripes[:, None, :] + near[None, :, :]
    bias = jnp.where(count > 0, jnp.log2(jnp.maximum(count, 1).astype(jnp.float32)), NEG)
    bias = bias.reshape(heads * blocks, block_total)

    query = query_rows.reshape(blocks, block_rows, heads, group, width)
    query = jnp.transpose(query, (2, 0, 3, 1, 4)).reshape(
        heads * blocks // PACK, PACK * group * block_rows, width
    )

    is_end = (ctx_index == 0) | (ctx_index == ctx_count - 1)
    opposite = jnp.where(ctx_index == 0, ctx_count - 1, 0)
    sources = [rep_index, ctx_index, jnp.where(is_end, opposite, -1)]
    for hop in range(1, ctx_count):
        sources.append(ctx_index - hop)
        sources.append(jnp.where(ctx_index + hop < ctx_count, ctx_index + hop, -1))
    sources = jnp.stack(sources).astype(jnp.int32)

    def call(units, kv, state, last=False):
        return attend_call(sources, bias, query, units, kv, state, last, scale)

    def swap(array):
        return lax.ppermute(array, "rep", [(0, 1), (1, 0)])

    both = (0, 1)
    state = call(((1, both),), (mine, half_of(1 - rep_index)), None)
    if ctx_count > 2:
        far = lax.ppermute(mine, "ctx", ends)
    final_hop = max(1, ctx_count - 2)
    for hop in range(1, final_hop + 1):
        here_left, here_right = from_left, from_right
        if hop < final_hop:
            from_left = lax.ppermute(here_left, "ctx", right)
            from_right = lax.ppermute(here_right, "ctx", left)
        elif ctx_count > 2:
            state = call(((2, both),), (far, swap(far)), state)
        slot = 1 + 2 * hop
        there_left = swap(here_left)
        there_right = swap(here_right)
        if hop < final_hop:
            kv = (here_left, there_left, here_right, there_right)
            state = call(((slot, both), (slot + 1, both)), kv, state)
        else:
            kv = (here_left, there_left, here_right, there_right)
            state = call(((slot, both), (slot + 1, both)), kv, state, True)
    out = state[0]
    out = out.reshape(heads, blocks, group, block_rows, width)
    return jnp.transpose(out, (1, 3, 0, 2, 4)).reshape(query_rows.shape)


def solution(mesh):
    in_specs = (
        P(("parts", "ctx"), "head", "rep", None),
        P(("parts", "ctx"), "head", None),
        P(("parts", "ctx"), "head", None),
        P("parts"),
        P("parts", None),
        P("parts"),
        P(("parts", "head"), None),
    )
    out_specs = P(("parts", "ctx"), "head", "rep", None)
    return jax.shard_map(run, mesh=mesh, in_specs=in_specs, out_specs=out_specs, check_vma=False)
```

time: 75.5 us -> 70.9 us (0.939)
  Pallas kernels: 29.5 us -> 24 us
  waiting for transfers between devices: 14 us -> 16 us
  starting transfers between devices: 22.6 us -> 21.7 us
    pallas_call x4, Pallas kernels: 29.5 us -> 24 us  [attend_call(): pl.pallas_call(functools.partial(attend_kernel, units, kv[0].shape[1], fi...]
    ppermute x5, waiting for transfers between devices: 14 us -> 16 us  [the longest x1 8.44 us: run(): far = lax.ppermute(mine, 'ctx', ends)]
    ppermute x5, starting transfers between devices: 6.02 us -> 4.87 us  [swap(): return lax.ppermute(array, 'rep', [(0, 1), (1, 0)])]
  transfers between devices with their start and end apart: 10 -> 10, of which waited for: 3 -> 2; matrix products, arithmetic and copies ran while one was open for 6% -> 6% of each run, Pallas kernels for 24% -> 22%
where the time goes in v3:
time: 70.9 us; the launch traced here: 70.6 us
  Pallas kernels  24 us (34%)
  starting transfers between devices  21.7 us (31%)
  waiting for transfers between devices  16 us (23%)
  local copies, waits for them, and re-layouts  7.13 us (10%)
  other arithmetic  1.43 us (2%)
    pallas_call x4, Pallas kernels, attend_call(): pl.pallas_call(functools.partial(attend_kernel, units, kv[0].shape[1], fi...  24 us
    ppermute x1, waiting for transfers between devices, run(): far = lax.ppermute(mine, 'ctx', ends)  8.44 us
    ppermute x1, waiting for transfers between devices, run(): from_right = lax.ppermute(here_right, 'ctx', left)  7.58 us
    ppermute x1, starting transfers between devices, run(): far = lax.ppermute(mine, 'ctx', ends)  6 us
    ppermute x5, starting transfers between devices, swap(): return lax.ppermute(array, 'rep', [(0, 1), (1, 0)])  4.87 us
    ppermute x1, starting transfers between devices, run(): from_left = lax.ppermute(mine, 'ctx', right)  4.82 us
    ppermute x1, starting transfers between devices, run(): from_left = lax.ppermute(here_left, 'ctx', right)  3.49 us
    transpose x1, local copies, waits for them, and re-layouts, run(): return jnp.transpose(out, (1, 3, 0, 2, 4)).reshape(query_rows.shape)  2.36 us
  transfers between devices with their start and end apart: 10, of which 2 were waited for; matrix products, arithmetic and copies ran while one was open for 6% of the time, Pallas kernels for 22%

profile of v3, /device:TPU:1, one launch (start us, length us, event | category | flops | bytes accessed | tf_op | source)
XLA Modules:
  0.0 70.6 jit_solution(5594188545299665402)
XLA Ops:
  0.0 1.6 %constant_dynamic-slice_fusion = (bf16[256,4,128]{2,1,0:T(4,128)(2,1)S(1)}, bf16[256,4,128]{2,1,0:T(4,128)(2,1)S(1)}, bf16[256,4,128]{2,1,0:T(4,128)(2,1)S(1)}, bf16[256,4,128]{2,1,0:T(4,128)(2,1)S(1)}) fusion(bf16[512,4,128]{2,1,0:T(4,128)(2,1)} %param.9, s32[]{:T(128)S(6)} %select_n.55, s32[]{:T(128)S(6)} %select_n.54, bf16[512,4,128]{2,1,0:T(4,128)(2,1)} %param.8), kind=kLoop, calls=%fused_computation.27 | loop fusion | bytes 2097160 | tf_op jit(solution)/shard_map/dynamic_slice | solution.py:200
  1.6 0.2 copy.25
  1.9 4.8 %collective-permute-start = (bf16[2,4,256,128]{3,2,1,0:T(8,128)(2,1)S(1)}, bf16[2,4,256,128]{3,2,1,0:T(8,128)(2,1)}, u32[]{:S(2)}, u32[]{:S(2)}) collective-permute-start(bf16[2,4,256,128]{3,2,1,0:T(8,128)(2,1)S(1)} %pad_maximum_fusion.refs_3_), channel_id=1, source_target_pairs={{0,4},{4,8},{8,12},{1,5},{5,9},{9,13},{2,6},{6,10},{10,14},{3,7},{... | collective-permute-start | bytes 1572872 | tf_op jit(solution)/shard_map/ppermute | solution.py:210
  6.8 1.3 %collective-permute-start.3 = (bf16[2,4,256,128]{3,2,1,0:T(8,128)(2,1)S(1)}, bf16[2,4,256,128]{3,2,1,0:T(8,128)(2,1)}, u32[]{:S(2)}, u32[]{:S(2)}) collective-permute-start(bf16[2,4,256,128]{3,2,1,0:T(8,128)(2,1)S(1)} %pad_maximum_fusion.refs_3_), channel_id=1, source_target_pairs={{4,0},{8,4},{12,8},{5,1},{9,5},{13,9},{6,2},{10,6},{14,10},{7,3},{... | collective-permute-start | bytes 1572872 | tf_op jit(solution)/shard_map/ppermute | solution.py:211
  8.0 6.0 %collective-permute-start.6 = (bf16[2,4,256,128]{3,2,1,0:T(8,128)(2,1)S(1)}, bf16[2,4,256,128]{3,2,1,0:T(8,128)(2,1)S(1)}, u32[]{:S(2)}, u32[]{:S(2)}) collective-permute-start(bf16[2,4,256,128]{3,2,1,0:T(8,128)(2,1)S(1)} %pad_maximum_fusion.refs_3_), channel_id=1, source_target_pairs={{0,12},{12,0},{1,13},{13,1},{2,14},{14,2},{3,15},{15,3},{16,28},{2... | collective-permute-start | bytes 1572872 | tf_op jit(solution)/shard_map/ppermute | solution.py:251
  14.1 0.2 copy.28
  14.3 0.7 %copy.36 = bf16[256,4,128]{2,0,1:T(8,128)(2,1)} copy(bf16[256,4,128]{2,1,0:T(4,128)(2,1)S(1)} %get-tuple-element.24) | data formatting | bytes 524288
  15.2 1.8 %copy.22 = bf16[4,128,4,3,128]{4,1,3,0,2:T(8,128)(2,1)S(1)} copy(bf16[4,128,4,3,128]{4,2,3,1,0:T(4,128)(2,1)} %bitcast.45) | data formatting | bytes 3145728 | tf_op jit(solution)/shard_map/reshape | solution.py:229
  17.0 1.0 %pad_maximum_fusion.1.refs_4_ = bf16[2,4,256,128]{3,2,1,0:T(8,128)(2,1)S(1)} fusion(bf16[1,4,256,128]{3,2,1,0:T(8,128)(2,1)S(1)} %bitcast.48, bf16[1,4,256,128]{3,2,1,0:T(8,128)(2,1)} %bitcast.49), kind=kLoop, calls=%fused_computation.1 | loop fusion | flops 262144 | bytes 1048576 | tf_op jit(solution)/shard_map/stack | solution.py:204
  18.2 0.1 multiply_reduce_fusion
  18.4 1.6 %collective-permute-start.8 = (bf16[2,4,256,128]{3,2,1,0:T(8,128)(2,1)}, bf16[2,4,256,128]{3,2,1,0:T(8,128)(2,1)S(1)}, u32[]{:S(2)}, u32[]{:S(2)}) collective-permute-start(bf16[2,4,256,128]{3,2,1,0:T(8,128)(2,1)} %collective-permute-done.refs_3_), channel_id=1, source_target_pairs={{0,1},{1,0},{2,3},{3,2},{4,5},{5,4},{6,7},{7,6},{8,9},{9,8},{10,11... | collective-permute-start | bytes 1572872 | tf_op jit(solution)/shard_map/ppermute | solution.py:246
  20.0 3.5 %collective-permute-start.1 = (bf16[2,4,256,128]{3,2,1,0:T(8,128)(2,1)}, bf16[2,4,256,128]{3,2,1,0:T(8,128)(2,1)S(1)}, u32[]{:S(2)}, u32[]{:S(2)}) collective-permute-start(bf16[2,4,256,128]{3,2,1,0:T(8,128)(2,1)} %collective-permute-done.refs_3_), channel_id=1, source_target_pairs={{0,4},{4,8},{8,12},{1,5},{5,9},{9,13},{2,6},{6,10},{10,14},{3,7},{... | collective-permute-start | bytes 1572872 | tf_op jit(solution)/shard_map/ppermute | solution.py:256
  23.5 0.3 collective-permute-start.9
  23.8 1.3 %collective-permute-start.4 = (bf16[2,4,256,128]{3,2,1,0:T(8,128)(2,1)}, bf16[2,4,256,128]{3,2,1,0:T(8,128)(2,1)S(1)}, u32[]{:S(2)}, u32[]{:S(2)}) collective-permute-start(bf16[2,4,256,128]{3,2,1,0:T(8,128)(2,1)} %collective-permute-done.3.refs_5_), channel_id=1, source_target_pairs={{4,0},{8,4},{12,8},{5,1},{9,5},{13,9},{6,2},{10,6},{14,10},{7,3},{... | collective-permute-start | bytes 1572872 | tf_op jit(solution)/shard_map/ppermute | solution.py:257
  25.2 8.4 %collective-permute-done.6.refs_3_ = bf16[2,4,256,128]{3,2,1,0:T(8,128)(2,1)S(1)} collective-permute-done((bf16[2,4,256,128]{3,2,1,0:T(8,128)(2,1)S(1)}, bf16[2,4,256,128]{3,2,1,0:T(8,128)(2,1)S(1)}, u32[]{:S(2)}, u32[]{:S(2)}) %collective-permute-start.6) | collective-permute-done | bytes 524320 | tf_op jit(solution)/shard_map/ppermute | solution.py:251
  33.7 1.8 %collective-permute-start.7 = (bf16[2,4,256,128]{3,2,1,0:T(8,128)(2,1)S(1)}, bf16[2,4,256,128]{3,2,1,0:T(8,128)(2,1)S(1)}, u32[]{:S(2)}, u32[]{:S(2)}) collective-permute-start(bf16[2,4,256,128]{3,2,1,0:T(8,128)(2,1)S(1)} %collective-permute-done.6.refs_3_), channel_id=1, source_target_pairs={{0,1},{1,0},{2,3},{3,2},{4,5},{5,4},{6,7},{7,6},{8,9},{9,8},{10,11... | collective-permute-start | bytes 1572872 | tf_op jit(solution)/shard_map/ppermute | solution.py:246
  35.5 4.9 %shard_map.73 = (f32[8,136,768]{2,1,0:T(8,128)S(1)}, f32[8,8,768]{2,1,0:T(8,128)S(1)}) custom-call(s32[9]{0:T(128)S(1)} %stack.51.refs_0_, f32[16,16]{1,0:T(8,128)S(1)} %bitcast.41, bf16[8,768,128]{2,1,0:T(8,128)(2,1)S(1)} %bitcast.36, bf16[2,4,256,128]{3,2,1,0:T(8,128)(2,1)S(1)} %pad_maximum_fusion.refs_3_, ...), custom_call_target="tpu_custom_call" | custom-call | flops 2415919104 | bytes 3145728 | tf_op jit(solution)/shard_map/pallas_call | solution.py:174
  40.4 0.3 collective-permute-start.2
  40.7 7.6 %collective-permute-done.4.refs_5_ = bf16[2,4,256,128]{3,2,1,0:T(8,128)(2,1)S(1)} collective-permute-done((bf16[2,4,256,128]{3,2,1,0:T(8,128)(2,1)}, bf16[2,4,256,128]{3,2,1,0:T(8,128)(2,1)S(1)}, u32[]{:S(2)}, u32[]{:S(2)}) %collective-permute-start.4) | collective-permute-done | bytes 524320 | tf_op jit(solution)/shard_map/ppermute | solution.py:257
  48.3 0.8 %collective-permute-start.5 = (bf16[2,4,256,128]{3,2,1,0:T(8,128)(2,1)S(1)}, bf16[2,4,256,128]{3,2,1,0:T(8,128)(2,1)S(1)}, u32[]{:S(2)}, u32[]{:S(2)}) collective-permute-start(bf16[2,4,256,128]{3,2,1,0:T(8,128)(2,1)S(1)} %collective-permute-done.4.refs_5_), channel_id=1, source_target_pairs={{0,1},{1,0},{2,3},{3,2},{4,5},{5,4},{6,7},{7,6},{8,9},{9,8},{10,11... | collective-permute-start | bytes 1572872 | tf_op jit(solution)/shard_map/ppermute | solution.py:246
  49.1 5.5 %shard_map.74 = (f32[8,136,768]{2,1,0:T(8,128)S(1)}, f32[8,8,768]{2,1,0:T(8,128)S(1)}) custom-call(s32[9]{0:T(128)S(1)} %stack.51.refs_0_, f32[16,16]{1,0:T(8,128)S(1)} %bitcast.42, bf16[8,768,128]{2,1,0:T(8,128)(2,1)S(1)} %bitcast.37, bf16[2,4,256,128]{3,2,1,0:T(8,128)(2,1)} %collective-permute-done.refs_3_, ...), custom_call_target="tpu_custom_call" | custom-call | flops 4831838208 | bytes 3145728 | tf_op jit(solution)/shard_map/pallas_call | solution.py:174
  54.6 5.0 %shard_map.75 = (f32[8,136,768]{2,1,0:T(8,128)S(1)}, f32[8,8,768]{2,1,0:T(8,128)S(1)}) custom-call(s32[9]{0:T(128)S(1)} %stack.51.refs_0_, f32[16,16]{1,0:T(8,128)S(1)} %bitcast.43, bf16[8,768,128]{2,1,0:T(8,128)(2,1)S(1)} %bitcast.38, bf16[2,4,256,128]{3,2,1,0:T(8,128)(2,1)S(1)} %collective-permute-done.6.refs_3_, ...), custom_call_target="tpu_custom_call" | custom-call | flops 2415919104 | bytes 3145728 | tf_op jit(solution)/shard_map/pallas_call | solution.py:174
  59.6 8.6 %shard_map.76 = (bf16[8,768,128]{2,1,0:T(8,128)(2,1)S(1)}, f32[8,136,768]{2,1,0:T(8,128)}, f32[8,8,768]{2,1,0:T(8,128)}) custom-call(s32[9]{0:T(128)S(1)} %stack.51.refs_0_, f32[16,16]{1,0:T(8,128)S(1)} %bitcast.44, bf16[8,768,128]{2,1,0:T(8,128)(2,1)S(1)} %bitcast.39, bf16[2,4,256,128]{3,2,1,0:T(8,128)(2,1)S(1)} %collective-permute-done.1.refs_3_, ...), custom_call_target="tpu_custom_call" | custom-call | flops 4831838208 | bytes 3145728 | tf_op jit(solution)/shard_map/pallas_call | solution.py:174
  68.2 2.4 %copy.29 = bf16[4,128,4,3,128]{4,2,3,1,0:T(4,128)(2,1)} copy(bf16[4,128,4,3,128]{4,1,3,0,2:T(8,128)(2,1)S(1)} %bitcast.40) | data formatting | bytes 3145728 | tf_op jit(solution)/shard_map/transpose | solution.py:271
  (29 shorter events, 0.7 us)
Async XLA Ops:
  0.0 15.1 %copy-start.2 = (s32[16]{0:T(128)S(1)}, s32[16]{0:T(128)}, u32[]{:S(2)}) copy-start(s32[16]{0:T(128)} %param.10) | copy-start | bytes 196
  0.0 15.2 %copy-start.3 = (s32[16]{0:T(128)S(1)}, s32[16]{0:T(128)}, u32[]{:S(2)}) copy-start(s32[16]{0:T(128)} %param.12) | copy-start | bytes 196
  1.9 16.2 %copy-start.1 = (s32[16,4]{0,1:T(4,128)S(1)}, s32[16,4]{0,1:T(4,128)}, u32[]{:S(2)}) copy-start(s32[16,4]{0,1:T(4,128)} %param.11) | copy-start | bytes 772
  1.9 16.5 %copy-start = (s32[4,4]{1,0:T(4,128)S(1)}, s32[4,4]{1,0:T(4,128)}, u32[]{:S(2)}) copy-start(s32[4,4]{1,0:T(4,128)} %param.13) | copy-start | bytes 196
  1.9 16.4 %collective-permute-start = (bf16[2,4,256,128]{3,2,1,0:T(8,128)(2,1)S(1)}, bf16[2,4,256,128]{3,2,1,0:T(8,128)(2,1)}, u32[]{:S(2)}, u32[]{:S(2)}) collective-permute-start(bf16[2,4,256,128]{3,2,1,0:T(8,128)(2,1)S(1)} %pad_maximum_fusion.refs_3_), channel_id=1, source_target_pairs={{0,4},{4,8},{8,12},{1,5},{5,9},{9,13},{2,6},{6,10},{10,14},{3,7},{... | collective-permute-start | bytes 1572872 | tf_op jit(solution)/shard_map/ppermute | solution.py:210
  6.8 16.7 %collective-permute-start.3 = (bf16[2,4,256,128]{3,2,1,0:T(8,128)(2,1)S(1)}, bf16[2,4,256,128]{3,2,1,0:T(8,128)(2,1)}, u32[]{:S(2)}, u32[]{:S(2)}) collective-permute-start(bf16[2,4,256,128]{3,2,1,0:T(8,128)(2,1)S(1)} %pad_maximum_fusion.refs_3_), channel_id=1, source_target_pairs={{4,0},{8,4},{12,8},{5,1},{9,5},{13,9},{6,2},{10,6},{14,10},{7,3},{... | collective-permute-start | bytes 1572872 | tf_op jit(solution)/shard_map/ppermute | solution.py:211
  8.0 25.6 %collective-permute-start.6 = (bf16[2,4,256,128]{3,2,1,0:T(8,128)(2,1)S(1)}, bf16[2,4,256,128]{3,2,1,0:T(8,128)(2,1)S(1)}, u32[]{:S(2)}, u32[]{:S(2)}) collective-permute-start(bf16[2,4,256,128]{3,2,1,0:T(8,128)(2,1)S(1)} %pad_maximum_fusion.refs_3_), channel_id=1, source_target_pairs={{0,12},{12,0},{1,13},{13,1},{2,14},{14,2},{3,15},{15,3},{16,28},{2... | collective-permute-start | bytes 1572872 | tf_op jit(solution)/shard_map/ppermute | solution.py:251
  18.4 30.7 %collective-permute-start.8 = (bf16[2,4,256,128]{3,2,1,0:T(8,128)(2,1)}, bf16[2,4,256,128]{3,2,1,0:T(8,128)(2,1)S(1)}, u32[]{:S(2)}, u32[]{:S(2)}) collective-permute-start(bf16[2,4,256,128]{3,2,1,0:T(8,128)(2,1)} %collective-permute-done.refs_3_), channel_id=1, source_target_pairs={{0,1},{1,0},{2,3},{3,2},{4,5},{5,4},{6,7},{7,6},{8,9},{9,8},{10,11... | collective-permute-start | bytes 1572872 | tf_op jit(solution)/shard_map/ppermute | solution.py:246
  20.0 20.4 %collective-permute-start.1 = (bf16[2,4,256,128]{3,2,1,0:T(8,128)(2,1)}, bf16[2,4,256,128]{3,2,1,0:T(8,128)(2,1)S(1)}, u32[]{:S(2)}, u32[]{:S(2)}) collective-permute-start(bf16[2,4,256,128]{3,2,1,0:T(8,128)(2,1)} %collective-permute-done.refs_3_), channel_id=1, source_target_pairs={{0,4},{4,8},{8,12},{1,5},{5,9},{9,13},{2,6},{6,10},{10,14},{3,7},{... | collective-permute-start | bytes 1572872 | tf_op jit(solution)/shard_map/ppermute | solution.py:256
  23.5 25.6 %collective-permute-start.9 = (bf16[2,4,256,128]{3,2,1,0:T(8,128)(2,1)}, bf16[2,4,256,128]{3,2,1,0:T(8,128)(2,1)S(1)}, u32[]{:S(2)}, u32[]{:S(2)}) collective-permute-start(bf16[2,4,256,128]{3,2,1,0:T(8,128)(2,1)} %collective-permute-done.3.refs_5_), channel_id=1, source_target_pairs={{0,1},{1,0},{2,3},{3,2},{4,5},{5,4},{6,7},{7,6},{8,9},{9,8},{10,11... | collective-permute-start | bytes 1572872 | tf_op jit(solution)/shard_map/ppermute | solution.py:246
  23.8 24.5 %collective-permute-start.4 = (bf16[2,4,256,128]{3,2,1,0:T(8,128)(2,1)}, bf16[2,4,256,128]{3,2,1,0:T(8,128)(2,1)S(1)}, u32[]{:S(2)}, u32[]{:S(2)}) collective-permute-start(bf16[2,4,256,128]{3,2,1,0:T(8,128)(2,1)} %collective-permute-done.3.refs_5_), channel_id=1, source_target_pairs={{4,0},{8,4},{12,8},{5,1},{9,5},{13,9},{6,2},{10,6},{14,10},{7,3},{... | collective-permute-start | bytes 1572872 | tf_op jit(solution)/shard_map/ppermute | solution.py:257
  33.7 20.9 %collective-permute-start.7 = (bf16[2,4,256,128]{3,2,1,0:T(8,128)(2,1)S(1)}, bf16[2,4,256,128]{3,2,1,0:T(8,128)(2,1)S(1)}, u32[]{:S(2)}, u32[]{:S(2)}) collective-permute-start(bf16[2,4,256,128]{3,2,1,0:T(8,128)(2,1)S(1)} %collective-permute-done.6.refs_3_), channel_id=1, source_target_pairs={{0,1},{1,0},{2,3},{3,2},{4,5},{5,4},{6,7},{7,6},{8,9},{9,8},{10,11... | collective-permute-start | bytes 1572872 | tf_op jit(solution)/shard_map/ppermute | solution.py:246
  40.4 19.2 %collective-permute-start.2 = (bf16[2,4,256,128]{3,2,1,0:T(8,128)(2,1)S(1)}, bf16[2,4,256,128]{3,2,1,0:T(8,128)(2,1)S(1)}, u32[]{:S(2)}, u32[]{:S(2)}) collective-permute-start(bf16[2,4,256,128]{3,2,1,0:T(8,128)(2,1)S(1)} %collective-permute-done.1.refs_3_), channel_id=1, source_target_pairs={{0,1},{1,0},{2,3},{3,2},{4,5},{5,4},{6,7},{7,6},{8,9},{9,8},{10,11... | collective-permute-start | bytes 1572872 | tf_op jit(solution)/shard_map/ppermute | solution.py:246
  48.3 11.3 %collective-permute-start.5 = (bf16[2,4,256,128]{3,2,1,0:T(8,128)(2,1)S(1)}, bf16[2,4,256,128]{3,2,1,0:T(8,128)(2,1)S(1)}, u32[]{:S(2)}, u32[]{:S(2)}) collective-permute-start(bf16[2,4,256,128]{3,2,1,0:T(8,128)(2,1)S(1)} %collective-permute-done.4.refs_5_), channel_id=1, source_target_pairs={{0,1},{1,0},{2,3},{3,2},{4,5},{5,4},{6,7},{7,6},{8,9},{9,8},{10,11... | collective-permute-start | bytes 1572872 | tf_op jit(solution)/shard_map/ppermute | solution.py:246
